TPU v7x, 32 devices: a whole 2x2x4 slice. The times are simulated.
32 devices in a mesh: seq: 8 (over z, y), dp: 4 (over x, core).
Axes of the slice: x: 2, y: 2, z: 4, core: 2. Of those that a mesh axis runs over, the one named last changes fastest.
Arguments:
- conv_input: bfloat16 [4, 1024, 2816], P('dp', 'seq'), may hold values from -6 to 6
- dt_raw: bfloat16 [4, 1024, 40], P('dp', 'seq'), may hold values from -3 to 3
- packing: int32 [4, 32, 2], P('dp', 'seq'), may hold values from 0 to 3, as said below
- resets: int32 [4, 1024], P('dp', 'seq'), may hold values 0 or 1
- conv_weight: float32 [4, 2816], replicated, may hold values from -3 to 3
- conv_bias: float32 [2816], replicated, may hold values from -1.5 to 1.5
- dt_bias: float32 [40], replicated
- decay_rate: float32 [40], replicated, may hold values from 0.5 to 2
- skip_gain: float32 [40], replicated, may hold values from 0.5 to 1.5
- grad_out: bfloat16 [4, 1024, 2560], P('dp', 'seq'), may hold values from -6 to 6
Outputs:
- layer_out: bfloat16 [4, 1024, 2560], P('dp', 'seq')
- grad_input: bfloat16 [4, 1024, 2816], P('dp', 'seq')
- grad_dt_raw: bfloat16 [4, 1024, 40], P('dp', 'seq')
- grad_conv_weight: float32 [4, 2816], replicated
- grad_conv_bias: float32 [2816], replicated
- grad_dt_bias: float32 [40], replicated
- grad_decay_rate: float32 [40], replicated
- grad_skip_gain: float32 [40], replicated
Inputs may be any that keep to these rules, and one draw needn't show every extreme that they name: `packing`: entry 0 names a packed sequence, entry 1 a block slot below 4. Within one shard, the 4 blocks of one loader row go to 4 distinct packed sequences, one to each, and each packed sequence receives exactly 4 blocks into distinct slots.
All inputs are finite; a program needn't handle non-finite values. No bound on the sum of `resets` on one device may be relied on, other than what follows from the above.
Results may differ from a plain program's by a relative error of at most 0.01.
Values may be sent and summed in bfloat16 or wider, within the bound.
A program may use at most 192 MiB of HBM per device.

v0:
```python
import jax
import jax.numpy as jnp
from jax import lax
from jax.sharding import PartitionSpec as P

Q = 128


def shifted(x, axis, by):
    size = lax.axis_size(axis)
    pairs = [(i, i + by) for i in range(size) if 0 <= i + by < size]
    return lax.ppermute(x, axis, pairs)


def prefix(x, axis, combine, identity):
    size, place = (lax.axis_size(axis), lax.axis_index(axis))
    everything = jax.tree.map(
        lambda part, kind: lax.all_gather(part.astype(kind), axis), x, (jnp.bfloat16, jnp.bfloat16)
    )
    start = jax.tree.map(
        lambda part, zero: jnp.broadcast_to(jnp.asarray(zero, part.dtype), part.shape), x, identity
    )

    def step(k, before):
        reached = k < place
        new = combine(
            before, jax.tree.map(lambda part, own: part[k].astype(own.dtype), everything, x)
        )
        return jax.tree.map(lambda a, b: jnp.where(reached, a, b), new, before)

    return lax.fori_loop(0, size, step, start)


def carried_in(x, axis, join, neutral):
    count = lax.axis_size(axis)
    place = lax.axis_index(axis)
    ahead = count - 1 - place
    gathered = jax.tree.map(
        lambda a, kind: lax.all_gather(a.astype(kind), axis),
        x,
        jax.tree.map(lambda a: jnp.bfloat16 if a.dtype == jnp.float32 else a.dtype, x),
    )
    state = jax.tree.map(lambda a, e: jnp.zeros_like(a) + jnp.asarray(e, a.dtype), x, neutral)

    def one(step, state):
        source = count - 1 - step
        return join(
            state,
            jax.tree.map(
                lambda a, own: lax.dynamic_index_in_dim(a, source, 0, False).astype(own.dtype),
                gathered,
                x,
            ),
        )

    return lax.fori_loop(0, ahead, one, state)


def contract(form, left, right):
    return jnp.einsum(form, left, right, preferred_element_type=jnp.float32)


def conv_silu(row_data, prior_rows, prior_keep, keep_rows, conv_weight, conv_bias):
    n_taps = conv_weight.shape[0]
    length = row_data.shape[0]
    padded = jnp.concatenate([prior_rows, row_data], axis=0)
    keep_all = jnp.concatenate([prior_keep, keep_rows], axis=0)
    summed = conv_bias[None, :] + conv_weight[n_taps - 1][None, :] * row_data
    joined = jnp.ones((length,), jnp.float32)
    for offset in range(1, n_taps):
        joined = joined * keep_all[n_taps - offset : n_taps - offset + length]
        earlier = padded[n_taps - 1 - offset : n_taps - 1 - offset + length]
        summed = summed + conv_weight[n_taps - 1 - offset][None, :] * earlier * joined[:, None]
    return jax.nn.silu(summed).astype(jnp.bfloat16)


def step_sizes(step_raw, dt_bias, decay_rate):
    step_size = jax.nn.softplus(step_raw + dt_bias[None, :])
    return (step_size, -step_size * decay_rate[None, :])


def split_inputs(activated, step_size, n_heads, head_size, n_state):
    inner_width = n_heads * head_size
    inputs_x = activated[..., :inner_width].reshape(activated.shape[:-1] + (n_heads, head_size))
    b_rows = activated[..., inner_width : inner_width + n_state]
    c_rows = activated[..., inner_width + n_state :]
    x_scaled = (inputs_x.astype(jnp.float32) * step_size[..., None]).astype(jnp.bfloat16)
    return (inputs_x, b_rows, c_rows, x_scaled)


def span_states(activated, step_size, log_decay, resets, n_heads, head_size, n_state):
    inputs_x, b_rows, c_rows, x_scaled = split_inputs(
        activated, step_size, n_heads, head_size, n_state
    )
    cum_decay = jnp.cumsum(log_decay, axis=1)
    segment = jnp.cumsum(resets, axis=1)
    alive = (segment == segment[:, -1:]).astype(jnp.float32)
    weights = jnp.exp(cum_decay[:, -1:, :] - cum_decay) * alive[:, :, None]
    x_weighted = (x_scaled.astype(jnp.float32) * weights[..., None]).astype(jnp.bfloat16)
    states = contract("cshp,csn->chpn", x_weighted, b_rows)
    decays = jnp.exp(cum_decay[:, -1, :]) * (segment[:, -1:] == 0).astype(jnp.float32)
    return (decays, states)


def entry_weights(activated, cum_decay, segment, n_state, inner_width):
    c_rows = activated[..., inner_width + n_state :]
    entry = jnp.exp(cum_decay) * (segment == 0).astype(jnp.float32)[..., None]
    return (c_rows.astype(jnp.float32)[:, :, None, :] * entry[..., None]).astype(jnp.bfloat16)


def carried_terms(c_decayed, starts):
    return contract("cthn,chpn->cthp", c_decayed, starts.astype(jnp.bfloat16))


def span_outputs(
    activated, step_size, log_decay, resets, starts, skip_gain, n_heads, head_size, n_state
):
    inputs_x, b_rows, c_rows, x_scaled = split_inputs(
        activated, step_size, n_heads, head_size, n_state
    )
    cum_decay = jnp.cumsum(log_decay, axis=1)
    segment = jnp.cumsum(resets, axis=1)
    span_len = activated.shape[1]
    scores = contract("ctn,csn->cts", c_rows, b_rows)
    position = jnp.arange(span_len)
    causal = position[:, None] >= position[None, :]
    allowed = causal[None] & (segment[:, :, None] == segment[:, None, :])
    cum_heads = jnp.swapaxes(cum_decay, 1, 2)
    exponent = cum_heads[:, :, :, None] - cum_heads[:, :, None, :]
    mask_heads = allowed[:, None]
    decay_matrix = jnp.where(mask_heads, jnp.exp(jnp.where(mask_heads, exponent, 0.0)), 0.0)
    mixing = (scores[:, None] * decay_matrix).astype(jnp.bfloat16)
    within = contract("chts,cshp->cthp", mixing, x_scaled)
    c_decayed = entry_weights(activated, cum_decay, segment, n_state, n_heads * head_size)
    summed = (
        within
        + carried_terms(c_decayed, starts)
        + skip_gain[None, None, :, None] * inputs_x.astype(jnp.float32)
    )
    return summed.astype(jnp.bfloat16)


def span_starts(decays, states, incoming):
    running = incoming
    starts = []
    for number in range(decays.shape[0]):
        starts.append(running)
        running = decays[number][:, None, None] * running + states[number]
    return jnp.stack(starts)


def device_summary(decays, states):
    total_decay = decays[0]
    total_state = states[0]
    for number in range(1, decays.shape[0]):
        total_decay = total_decay * decays[number]
        total_state = decays[number][:, None, None] * total_state + states[number]
    return (total_decay, total_state)


def join_segments(earlier, latter):
    first_decay, first_state = earlier
    next_decay, next_state = latter
    return (first_decay * next_decay, next_decay[:, None, None] * first_state + next_state)


def per_device(
    conv_input,
    dt_raw,
    packing,
    resets,
    conv_weight,
    conv_bias,
    dt_bias,
    decay_rate,
    skip_gain,
    grad_out,
):
    groups = lax.axis_size("dp")
    length = conv_input.shape[1]
    channels = conv_input.shape[2]
    n_heads = dt_raw.shape[2]
    inner_width = grad_out.shape[2]
    head_size = inner_width // n_heads
    n_state = (channels - inner_width) // 2
    n_taps = conv_weight.shape[0]
    n_held = packing.shape[1]
    block_len = length // n_held
    span_len = Q
    nchunks = length // span_len
    target = packing[0, :, 0]
    slot_index = packing[0, :, 1]
    chooser = (target[None, :] == jnp.arange(groups, dtype=jnp.int32)[:, None]).astype(jnp.bfloat16)
    rows_in = conv_input[0].reshape(n_held, block_len, channels)
    steps_in = dt_raw[0].reshape(n_held, block_len, n_heads)
    send_rows = jnp.einsum("gj,jbc->gbc", chooser, rows_in, preferred_element_type=jnp.bfloat16)
    send_steps = jnp.einsum("gj,jbh->gbh", chooser, steps_in, preferred_element_type=jnp.bfloat16)
    send_tag = jnp.dot(
        chooser, (slot_index + 1).astype(jnp.bfloat16), preferred_element_type=jnp.float32
    ).astype(jnp.bfloat16)
    got_rows, got_steps, got_tag = (
        lax.all_to_all(send_rows, "dp", split_axis=0, concat_axis=0, tiled=True),
        lax.all_to_all(send_steps, "dp", split_axis=0, concat_axis=0, tiled=True),
        lax.all_to_all(send_tag, "dp", split_axis=0, concat_axis=0, tiled=True),
    )
    slot_marks = jnp.arange(1, n_held + 1).astype(jnp.bfloat16)
    placer = (got_tag[None, :] == slot_marks[:, None]).astype(jnp.bfloat16)
    packed = jnp.einsum(
        "kg,gbc->kbc", placer, got_rows, preferred_element_type=jnp.bfloat16
    ).reshape(length, channels)
    packed_steps = jnp.einsum(
        "kg,gbh->kbh", placer, got_steps, preferred_element_type=jnp.bfloat16
    ).reshape(length, n_heads)
    resets_here = resets[0]
    keep_rows = (1 - resets_here).astype(jnp.float32)
    tail_rows = packed[length - n_taps + 1 :]
    tail_keep = keep_rows[length - n_taps + 1 :].astype(jnp.bfloat16)
    prior_rows, prior_flag = shifted((tail_rows, tail_keep), "seq", 1)
    prior_keep = prior_flag.astype(jnp.float32)
    span_resets = resets_here.reshape(nchunks, span_len)

    def front_section(rows_f, prior_f, steps_f, weight, bias, step_bias, rate):
        activated = conv_silu(rows_f, prior_f, prior_keep, keep_rows, weight, bias)
        step_size, log_decay = step_sizes(steps_f, step_bias, rate)
        decays, states = span_states(
            activated.reshape(nchunks, span_len, channels),
            step_size.reshape(nchunks, span_len, n_heads),
            log_decay.reshape(nchunks, span_len, n_heads),
            span_resets,
            n_heads,
            head_size,
            n_state,
        )
        return (activated, step_size, decays, states)

    front_out, front_pull = jax.vjp(
        front_section,
        packed.astype(jnp.float32),
        prior_rows.astype(jnp.float32),
        packed_steps.astype(jnp.float32),
        conv_weight,
        conv_bias,
        dt_bias,
        decay_rate,
    )
    activated, step_size, decays, states = front_out
    summary, summary_pull = jax.vjp(device_summary, decays, states)
    total_decay, total_state = summary
    identity = (jnp.ones_like(total_decay), jnp.zeros_like(total_state))
    incoming = prefix((total_decay, total_state), "seq", join_segments, identity)[1]

    def back_section(act_in, size_in, decays_in, states_in, entering, gain, rate):
        log_decay = -size_in * rate[None, :]
        starts = span_starts(decays_in, states_in, entering)
        result = span_outputs(
            act_in.reshape(nchunks, span_len, channels),
            size_in.reshape(nchunks, span_len, n_heads),
            log_decay.reshape(nchunks, span_len, n_heads),
            span_resets,
            starts,
            gain,
            n_heads,
            head_size,
            n_state,
        )
        return result.reshape(length, inner_width)

    cotangent = grad_out[0]
    layer_out, back_pull = jax.vjp(
        back_section, activated, step_size, decays, states, incoming, skip_gain, decay_rate
    )
    grad_act, grad_size, grad_decays, grad_states, grad_entering, grad_gain, grad_rate_back = (
        back_pull(cotangent)
    )
    after_grad = carried_in((total_decay, grad_entering), "seq", join_segments, identity)[1]
    decay_grad = jnp.sum(after_grad * incoming, axis=(1, 2))
    summary_decays, summary_states = summary_pull((decay_grad, after_grad))
    grad_rows, grad_prior, grad_steps, grad_weight, grad_bias, grad_step_bias, grad_rate_front = (
        front_pull(
            (grad_act, grad_size, grad_decays + summary_decays, grad_states + summary_states)
        )
    )
    spill_rows = shifted(grad_prior.astype(jnp.bfloat16), "seq", -1).astype(grad_prior.dtype)
    grad_rows = jnp.concatenate(
        [grad_rows[: length - n_taps + 1], grad_rows[length - n_taps + 1 :] + spill_rows], axis=0
    )
    back_rows = jnp.einsum(
        "kg,kbc->gbc",
        placer,
        grad_rows.astype(jnp.bfloat16).reshape(n_held, block_len, channels),
        preferred_element_type=jnp.bfloat16,
    )
    back_steps = jnp.einsum(
        "kg,kbh->gbh",
        placer,
        grad_steps.astype(jnp.bfloat16).reshape(n_held, block_len, n_heads),
        preferred_element_type=jnp.bfloat16,
    )
    ret_rows, ret_steps = (
        lax.all_to_all(back_rows, "dp", split_axis=0, concat_axis=0, tiled=True),
        lax.all_to_all(back_steps, "dp", split_axis=0, concat_axis=0, tiled=True),
    )
    grad_input = jnp.einsum(
        "gj,gbc->jbc", chooser, ret_rows, preferred_element_type=jnp.bfloat16
    ).reshape(1, length, channels)
    grad_dt = jnp.einsum(
        "gj,gbh->jbh", chooser, ret_steps, preferred_element_type=jnp.bfloat16
    ).reshape(1, length, n_heads)
    gradients = lax.psum(
        (grad_weight, grad_bias, grad_step_bias, grad_rate_front + grad_rate_back, grad_gain),
        ("seq", "dp"),
    )
    return (
        layer_out[None],
        grad_input,
        grad_dt,
        gradients[0],
        gradients[1],
        gradients[2],
        gradients[3],
        gradients[4],
    )


def solution(mesh):
    in_specs = (
        P("dp", "seq", None),
        P("dp", "seq", None),
        P("dp", "seq", None),
        P("dp", "seq"),
        P(),
        P(),
        P(),
        P(),
        P(),
        P("dp", "seq", None),
    )
    out_specs = (
        P("dp", "seq", None),
        P("dp", "seq", None),
        P("dp", "seq", None),
        P(),
        P(),
        P(),
        P(),
        P(),
    )
    return jax.shard_map(
        per_device, mesh=mesh, in_specs=in_specs, out_specs=out_specs, check_vma=False
    )
```

profile of v0, /device:TPU:0, one launch (start us, length us, event | category | flops | bytes accessed | tf_op | source)
XLA Modules:
  0.0 348.1 jit_solution(11199877150396958151)
XLA Ops:
  9.5 4.2 %all-to-all-start = ((bf16[4,1,1]{2,1,0:T(2,128)(2,1)}), bf16[4,1,1]{2,1,0:T(2,128)(2,1)S(1)}, u32[]{:S(2)}, u32[]{:S(2)}) async-start(bf16[4,1,1]{2,1,0:T(2,128)(2,1)} %copy.248), calls=%async_computation | async-start | bytes 4096 | tf_op jit(solution)/shard_map/all_to_all | solution.py:204
  14.4 3.9 %collective-permute-start.1 = (bf16[3]{0:T(256)(128)(2,1)S(1)}, bf16[3]{0:T(256)(128)(2,1)S(1)}, u32[]{:S(2)}, u32[]{:S(2)}) collective-permute-start(bf16[3]{0:T(256)(128)(2,1)S(1)} %slice_bitcast_fusion.3), channel_id=1, source_target_pairs={{0,4},{4,8},{8,12},{12,16},{16,20},{20,24},{24,28},{1,5},{5,9},{9,... | collective-permute-start | bytes 26 | tf_op jit(solution)/shard_map/ppermute | solution.py:12
  18.3 1.0 reduce_window_sum.43
  23.1 1.7 slice_reduce_fusion.3
  24.8 1.4 copy.274
  28.2 3.3 all-to-all-start.2
  32.2 3.1 all-to-all-done.2
  35.3 3.5 %all-to-all-start.1 = ((bf16[4,32,2816]{2,1,0:T(8,128)(2,1)}), bf16[4,32,2816]{2,1,0:T(8,128)(2,1)S(1)}, u32[]{:S(2)}, u32[]{:S(2)}) async-start(bf16[4,32,2816]{2,1,0:T(8,128)(2,1)} %copy.251), calls=%async_computation.1 | async-start | bytes 1441792 | tf_op jit(solution)/shard_map/all_to_all | solution.py:202
  41.0 8.7 %all-to-all-done.1 = bf16[4,32,2816]{2,1,0:T(8,128)(2,1)S(1)} async-done(((bf16[4,32,2816]{2,1,0:T(8,128)(2,1)}), bf16[4,32,2816]{2,1,0:T(8,128)(2,1)S(1)}, u32[]{:S(2)}, u32[]{:S(2)}) %all-to-all-start.1) | async-done | bytes 720928 | tf_op jit(solution)/shard_map/all_to_all | solution.py:202
  50.8 3.6 %collective-permute-start = (bf16[3,2816]{1,0:T(4,128)(2,1)S(1)}, bf16[3,2816]{1,0:T(4,128)(2,1)S(1)}, u32[]{:S(2)}, u32[]{:S(2)}) collective-permute-start(bf16[3,2816]{1,0:T(4,128)(2,1)S(1)} %slice.88), channel_id=1, source_target_pairs={{0,4},{4,8},{8,12},{12,16},{16,20},{20,24},{24,28},{1,5},{5,9},{9,... | collective-permute-start | bytes 50696 | tf_op jit(solution)/shard_map/ppermute | solution.py:12
  54.5 1.3 collective-permute-done
  55.9 2.2 fusion.50
  58.2 2.0 fusion.35
  61.2 1.5 copy.271
  63.5 1.5 copy.269
  64.9 2.6 multiply_reduce_fusion.4
  67.9 1.2 convolution_convert_fusion.4
  69.2 20.4 %all-gather = bf16[8,1,40]{2,1,0:T(2,128)(2,1)S(1)} all-gather(bf16[1,1,40]{2,1,0:T(2,128)(2,1)S(1)} %copy-done.70), channel_id=2, replica_groups=mesh['seq'=8,'dp'=4] {'seq'}, dimensions={0}, use_global_device_ids=true | all-gather | bytes 720 | tf_op jit(solution)/shard_map/all_gather | solution.py:18
  91.1 1.2 slice_convert_fusion.1
  92.3 1.7 copy.255
  94.1 1.0 fusion.67
  95.1 3.7 %fusion.51 = (bf16[1,128,40,64]{1,3,2,0:T(8,128)(2,1)}, f32[1,128,40,64]{1,3,2,0:T(8,128)}) fusion(bf16[1,128,40,64]{1,3,2,0:T(8,128)(2,1)} %bitcast.294, f32[128,40]{0,1:T(8,128)S(1)} %copy-done.26, f32[40]{0:T(128)S(1)} %copy-done.72, bf16[40,64,128]{2,1,0:T(8,128)(2,1)} %bitcast.293, f32[40,128]{1,0:T(8,128)S(1)} %copy.266, f32[128,128]{0,1:T(8,128)S(1)} %fusion.67, ...), kind=kOutput, calls=%fused_computation.105 | convolution fusion | flops 89784320 | bytes 3399840 | tf_op jit(solution)/shard_map/transpose(jvp(chts,cshp->cthp))/dot_general | solution.py:60
  98.8 2.3 copy.277
  101.1 3.9 %fusion.9 = (f32[40,128]{1,0:T(8,128)}, f32[40,128]{1,0:T(8,128)}, bf16[128,128]{0,1:T(8,128)(2,1)S(1)}) fusion(f32[40,128]{1,0:T(8,128)S(1)} %copy.266, f32[128,128]{0,1:T(8,128)} %copy-done.39, pred[128,128]{0,1:T(8,128)(4,1)S(1)} %fusion.62, bf16[40,64,128]{2,1,0:T(8,128)(2,1)} %bitcast.295, f32[128,40,64]{0,2,1:T(8,128)S(1)} %bitcast.276, ...), kind=kOutput, calls=%fused_computation.20 | convolution fusion | flops 93034496 | bytes 2162688 | tf_op jit(solution)/shard_map/transpose(jvp(chts,cshp->cthp))/dot_general | solution.py:60
  105.0 1.5 fusion.38
  106.5 1.5 fusion.37
  108.0 2.1 fusion.33
  110.2 37.6 %all-gather.8.cloned.1.call-done = bf16[320,64,128]{2,1,0:T(8,128)(2,1)} async-done(((bf16[40,64,128]{2,1,0:T(8,128)(2,1)}), bf16[320,64,128]{2,1,0:T(8,128)(2,1)}) %all-gather.8.cloned.1.call-update) | async-done | bytes 5242896 | tf_op jit(solution)/shard_map/all_gather | solution.py:39
  147.9 10.3 %while.28 = (s32[]{:T(128)}, f32[40,64,128]{2,1,0:T(8,128)S(1)}, s32[]{:T(128)}, bf16[8,40]{1,0:T(8,128)(2,1)S(1)}, bf16[8,40,64,128]{3,2,1,0:T(8,128)(2,1)}, /*index=5*/s32[]{:T(128)}, s32[]{:T(128)}, s32[]{:T(128)}, s32[]{:T(128)}) while((s32[]{:T(128)}, f32[40,64,128]{2,1,0:T(8,128)S(1)}, s32[]{:T(128)}, bf16[8,40]{1,0:T(8,128)(2,1)S(1)}, ...), condition=%wide.region_7.8_spmd, body=%wide.region_6.7_spmd.sunk | while | flops 983086 | bytes 3277355 | solution.py:56
  148.0 1.4 convert_add_fusion.3
  149.4 1.4 convert_add_fusion.3
  150.8 1.4 convert_add_fusion.3
  152.3 1.4 convert_add_fusion.3
  153.7 1.4 convert_add_fusion.3
  155.2 1.5 convert_add_fusion.3
  156.7 1.5 convert_add_fusion.3
  158.8 3.9 %fusion.24 = (f32[128,40]{0,1:T(8,128)}, f32[128,40]{0,1:T(8,128)S(1)}, f32[128,40]{0,1:T(8,128)}, bf16[1,128,40,64]{1,3,2,0:T(8,128)(2,1)}) fusion(f32[1,128,40,64]{1,3,2,0:T(8,128)} %bitcast.278, f32[128,40]{0,1:T(8,128)S(1)} %copy-done.24, f32[128,40]{0,1:T(8,128)S(1)} %copy-done.26, f32[1,128,40,64]{1,3,2,0:T(8,128)} %get-tuple-element.319, ...), kind=kOutput, calls=%fused_computation.63 | convolution fusion | flops 88785920 | bytes 4722688 | tf_op jit(solution)/shard_map/transpose(jvp(cshp,csn->chpn))/dot_general | solution.py:60
  164.1 2.1 fusion.39
  166.2 68.2 %all-gather.6.cloned.1.call-done = bf16[320,64,128]{2,1,0:T(8,128)(2,1)} async-done(((bf16[40,64,128]{2,1,0:T(8,128)(2,1)}), bf16[320,64,128]{2,1,0:T(8,128)(2,1)}) %all-gather.6.cloned.1.call-update) | async-done | bytes 5242896 | tf_op jit(solution)/shard_map/all_gather | solution.py:18
  234.4 17.0 %while.29 = (s32[]{:T(128)}, f32[40,64,128]{2,1,0:T(8,128)S(1)}, s32[]{:T(128)}, bf16[8,40]{1,0:T(8,128)(2,1)}, bf16[8,40,64,128]{3,2,1,0:T(8,128)(2,1)}, /*index=5*/s32[]{:T(128)}, s32[]{:T(128)}) while((s32[]{:T(128)}, f32[40,64,128]{2,1,0:T(8,128)S(1)}, s32[]{:T(128)}, bf16[8,40]{1,0:T(8,128)(2,1)}, ...), condition=%wide.region_3.4_spmd.clone, body=%wide.region_2.3_spmd.clone.sunk | while | flops 1638444 | bytes 3277313 | solution.py:31
  235.1 1.4 fusion.139
  237.2 1.4 fusion.139
  239.3 1.4 fusion.139
  241.5 1.4 fusion.139
  243.6 1.4 fusion.139
  245.7 1.4 fusion.139
  247.8 1.4 fusion.139
  250.0 1.4 fusion.139
  252.5 1.3 fusion.2
  253.8 1.5 copy.275
  255.3 2.2 copy.278
  257.5 4.2 %multiply_reduce_fusion.3 = (f32[2816]{0:T(1024)}, f32[2816]{0:T(1024)}, f32[2816]{0:T(1024)}, f32[2816]{0:T(1024)}, f32[2816]{0:T(1024)}, /*index=5*/f32[128,2816]{1,0:T(8,128)S(1)}) fusion(f32[128,2816]{1,0:T(8,128)S(1)} %copy-done.2, f32[3,2816]{1,0:T(4,128)} %copy-done.16, f32[128]{0:T(128)S(1)} %get-tuple-element.302, f32[128]{0:T(128)} %get-tuple-element.303, ...), kind=kLoop, calls=%fused_computation.45 | loop fusion | flops 13682944 | bytes 6579712 | tf_op jit(solution)/shard_map/transpose(jvp())/reduce_sum | solution.py:73
  262.5 1.3 slice_add_fusion
  265.7 2.0 reduce_window_sum.46
  268.4 3.2 fusion.19
  271.7 2.3 copy.299
  276.9 0.9 fusion.61
  277.9 1.1 reduce_window_sum.47
  280.3 3.3 all-to-all-start.4
  283.5 1.3 collective-permute-start.2
  285.2 4.0 %collective-permute-done.2 = bf16[3,2816]{1,0:T(4,128)(2,1)S(1)} collective-permute-done((bf16[3,2816]{1,0:T(4,128)(2,1)S(1)}, bf16[3,2816]{1,0:T(4,128)(2,1)S(1)}, u32[]{:S(2)}, u32[]{:S(2)}) %collective-permute-start.2) | collective-permute-done | bytes 16928 | tf_op jit(solution)/shard_map/ppermute | solution.py:12
  291.0 3.5 %all-to-all-start.3 = ((bf16[4,32,2816]{2,1,0:T(8,128)(2,1)}), bf16[4,32,2816]{2,1,0:T(8,128)(2,1)S(1)}, u32[]{:S(2)}, u32[]{:S(2)}) async-start(bf16[4,32,2816]{2,1,0:T(8,128)(2,1)} %copy.280), calls=%async_computation.3 | async-start | bytes 1441792 | tf_op jit(solution)/shard_map/all_to_all | solution.py:300
  294.6 43.9 %all-reduce.15 = (f32[4,2816]{1,0:T(4,128)}, f32[2816]{0:T(1024)}, f32[40]{0:T(128)}, f32[40]{0:T(128)}, f32[40]{0:T(128)}) all-reduce(f32[4,2816]{1,0:T(4,128)S(1)} %pad_add_fusion.1, f32[2816]{0:T(1024)S(1)} %copy-done.41, f32[40]{0:T(128)S(1)} %get-tuple-element.272, ...), channel_id=1, replica_groups=mesh['seq'=8,'dp'=4] {'seq','dp'}, use_global_device_ids=true, to_apply=%region_22.23 | all-reduce | flops 14200 | bytes 113600 | tf_op jit(solution)/shard_map/psum | solution.py:309
  340.4 0.9 copy.282
  (265 shorter events, 36.1 us)
Async XLA Ops:
  7.2 19.0 %copy-start = (bf16[1,128,2816]{2,1,0:T(8,128)(2,1)S(1)}, bf16[1,128,2816]{2,1,0:T(8,128)(2,1)}, u32[]{:S(2)}) copy-start(bf16[1,128,2816]{2,1,0:T(8,128)(2,1)} %param.14) | copy-start | bytes 2162692
  7.9 19.2 %copy-start.76 = (s32[4]{0:T(128)}, s32[4]{0:T(128)S(1)}, u32[]{:S(2)}) copy-start(s32[4]{0:T(128)S(1)} %slice_bitcast_fusion.4) | copy-start | bytes 52
  9.5 18.7 %all-to-all-start = ((bf16[4,1,1]{2,1,0:T(2,128)(2,1)}), bf16[4,1,1]{2,1,0:T(2,128)(2,1)S(1)}, u32[]{:S(2)}, u32[]{:S(2)}) async-start(bf16[4,1,1]{2,1,0:T(2,128)(2,1)} %copy.248), calls=%async_computation | async-start | bytes 4096 | tf_op jit(solution)/shard_map/all_to_all | solution.py:204
  14.4 13.8 %copy-start.54 = (f32[128]{0:T(128)}, f32[128]{0:T(128)S(1)}, u32[]{:S(2)}) copy-start(f32[128]{0:T(128)S(1)} %get-tuple-element.317) | copy-start | bytes 1540
  14.4 13.7 %collective-permute-start.1 = (bf16[3]{0:T(256)(128)(2,1)S(1)}, bf16[3]{0:T(256)(128)(2,1)S(1)}, u32[]{:S(2)}, u32[]{:S(2)}) collective-permute-start(bf16[3]{0:T(256)(128)(2,1)S(1)} %slice_bitcast_fusion.3), channel_id=1, source_target_pairs={{0,4},{4,8},{8,12},{12,16},{16,20},{20,24},{24,28},{1,5},{5,9},{9,... | collective-permute-start | bytes 26 | tf_op jit(solution)/shard_map/ppermute | solution.py:12
  18.3 31.4 %copy-start.78 = (bf16[4]{0:T(256)(128)(2,1)}, bf16[4]{0:T(256)(128)(2,1)S(1)}, u32[]{:S(2)}) copy-start(bf16[4]{0:T(256)(128)(2,1)S(1)} %add_convert_fusion) | copy-start | bytes 28
  19.3 7.8 %copy-start.66 = (s32[1,128]{1,0:T(1,128)}, s32[1,128]{1,0:T(1,128)S(1)}, u32[]{:S(2)}) copy-start(s32[1,128]{1,0:T(1,128)S(1)} %reduce_window_sum.43) | copy-start | bytes 1540
  21.2 19.1 %copy-start.51 = (f32[128]{0:T(128)}, f32[128]{0:T(128)S(1)}, u32[]{:S(2)}) copy-start(f32[128]{0:T(128)S(1)} %get-tuple-element.314) | copy-start | bytes 1540
  21.2 19.1 %copy-start.64 = (f32[128]{0:T(128)}, f32[128]{0:T(128)S(1)}, u32[]{:S(2)}) copy-start(f32[128]{0:T(128)S(1)} %get-tuple-element.315) | copy-start | bytes 1540
  26.2 32.0 %copy-start.10 = (bf16[1,128,2560]{1,2,0:T(8,128)(2,1)}, bf16[1,128,2560]{1,2,0:T(8,128)(2,1)S(1)}, u32[]{:S(2)}) copy-start(bf16[1,128,2560]{1,2,0:T(8,128)(2,1)S(1)} %copy.274) | copy-start | bytes 1966084
  26.2 5.2 %copy-start.73 = (s32[1,128]{1,0:T(1,128)S(1)}, s32[1,128]{1,0:T(1,128)}, u32[]{:S(2)}) copy-start(s32[1,128]{1,0:T(1,128)} %param.17) | copy-start | bytes 1540
  27.1 12.2 %copy-start.59 = (f32[40]{0:T(128)S(1)}, f32[40]{0:T(128)}, u32[]{:S(2)}) copy-start(f32[40]{0:T(128)} %param.20) | copy-start | bytes 484
  27.2 12.2 %copy-start.62 = (f32[40]{0:T(128)S(1)}, f32[40]{0:T(128)}, u32[]{:S(2)}) copy-start(f32[40]{0:T(128)} %param.21) | copy-start | bytes 484
  28.2 7.1 %all-to-all-start.2 = ((bf16[4,2,640]{2,1,0:T(2,128)(2,1)}), bf16[4,2,640]{2,1,0:T(2,128)(2,1)S(1)}, u32[]{:S(2)}, u32[]{:S(2)}) async-start(bf16[4,2,640]{2,1,0:T(2,128)(2,1)} %reshape.951), calls=%async_computation.2 | async-start | bytes 20480 | tf_op jit(solution)/shard_map/all_to_all | solution.py:203
  32.2 18.4 %copy-start.74 = (bf16[4]{0:T(256)(128)(2,1)}, bf16[4]{0:T(256)(128)(2,1)S(1)}, u32[]{:S(2)}) copy-start(bf16[4]{0:T(256)(128)(2,1)S(1)} %reduce.18) | copy-start | bytes 28
  35.3 14.4 %all-to-all-start.1 = ((bf16[4,32,2816]{2,1,0:T(8,128)(2,1)}), bf16[4,32,2816]{2,1,0:T(8,128)(2,1)S(1)}, u32[]{:S(2)}, u32[]{:S(2)}) async-start(bf16[4,32,2816]{2,1,0:T(8,128)(2,1)} %copy.251), calls=%async_computation.1 | async-start | bytes 1441792 | tf_op jit(solution)/shard_map/all_to_all | solution.py:202
  38.8 109.0 %all-gather.8.cloned.1.call-start = ((), (), s32[]{:S(2)}) async-start(), calls=%async_computation.6 | async-start | bytes 5898240 | tf_op jit(solution)/shard_map/all_gather | solution.py:39
  39.8 10.9 %copy-start.17 = (f32[1,128,40]{1,2,0:T(8,128)}, f32[1,128,40]{1,2,0:T(8,128)S(1)}, u32[]{:S(2)}) copy-start(f32[1,128,40]{1,2,0:T(8,128)S(1)} %copy.270) | copy-start | bytes 61444
  40.3 10.4 %copy-start.57 = (f32[40]{0:T(128)}, f32[40]{0:T(128)S(1)}, u32[]{:S(2)}) copy-start(f32[40]{0:T(128)S(1)} %get-tuple-element.310) | copy-start | bytes 484
  50.7 5.2 %copy-start.6 = (bf16[4,32,2816]{2,1,0:T(8,128)(2,1)}, bf16[4,32,2816]{2,1,0:T(8,128)(2,1)S(1)}, u32[]{:S(2)}) copy-start(bf16[4,32,2816]{2,1,0:T(8,128)(2,1)S(1)} %copy.254) | copy-start | bytes 2162692
  50.7 5.2 %copy-start.29 = (f32[2816]{0:T(1024)S(1)}, f32[2816]{0:T(1024)}, u32[]{:S(2)}) copy-start(f32[2816]{0:T(1024)} %get-tuple-element.268) | copy-start | bytes 33796
  50.7 5.2 %copy-start.31 = (f32[2816]{0:T(1024)S(1)}, f32[2816]{0:T(1024)}, u32[]{:S(2)}) copy-start(f32[2816]{0:T(1024)} %get-tuple-element.269) | copy-start | bytes 33796
  50.7 5.2 %copy-start.33 = (f32[2816]{0:T(1024)S(1)}, f32[2816]{0:T(1024)}, u32[]{:S(2)}) copy-start(f32[2816]{0:T(1024)} %get-tuple-element.270) | copy-start | bytes 33796
  50.7 5.2 %copy-start.48 = (f32[2816]{0:T(1024)S(1)}, f32[2816]{0:T(1024)}, u32[]{:S(2)}) copy-start(f32[2816]{0:T(1024)} %param.19) | copy-start | bytes 33796
  50.7 5.2 %copy-start.49 = (f32[128]{0:T(128)S(1)}, f32[128]{0:T(128)}, u32[]{:S(2)}) copy-start(f32[128]{0:T(128)} %get-tuple-element.303) | copy-start | bytes 1540
  50.8 5.2 %copy-start.55 = (f32[128]{0:T(128)S(1)}, f32[128]{0:T(128)}, u32[]{:S(2)}) copy-start(f32[128]{0:T(128)} %copy-done.54) | copy-start | bytes 1540
  50.8 5.1 %collective-permute-start = (bf16[3,2816]{1,0:T(4,128)(2,1)S(1)}, bf16[3,2816]{1,0:T(4,128)(2,1)S(1)}, u32[]{:S(2)}, u32[]{:S(2)}) collective-permute-start(bf16[3,2816]{1,0:T(4,128)(2,1)S(1)} %slice.88), channel_id=1, source_target_pairs={{0,4},{4,8},{8,12},{12,16},{16,20},{20,24},{24,28},{1,5},{5,9},{9,... | collective-permute-start | bytes 50696 | tf_op jit(solution)/shard_map/ppermute | solution.py:12
  58.1 33.0 %copy-start.5 = (bf16[1,128,2816]{2,1,0:T(8,128)(2,1)}, bf16[1,128,2816]{2,1,0:T(8,128)(2,1)S(1)}, u32[]{:S(2)}) copy-start(bf16[1,128,2816]{2,1,0:T(8,128)(2,1)S(1)} %get-tuple-element.300) | copy-start | bytes 2162692
  58.2 31.5 %copy-start.12 = (f32[128,128]{1,0:T(8,128)}, f32[128,128]{1,0:T(8,128)S(1)}, u32[]{:S(2)}) copy-start(f32[128,128]{1,0:T(8,128)S(1)} %fusion.73) | copy-start | bytes 196612
  60.2 174.2 %all-gather.6.cloned.1.call-start = ((), (), s32[]{:S(2)}) async-start(), calls=%async_computation.5 | async-start | bytes 5898240 | tf_op jit(solution)/shard_map/all_gather | solution.py:18
  67.9 22.6 %copy-start.43 = (f32[2560]{0:T(1024)S(1)}, f32[2560]{0:T(1024)}, u32[]{:S(2)}) copy-start(f32[2560]{0:T(1024)} %get-tuple-element.307) | copy-start | bytes 30724
  94.0 14.0 %copy-start.3 = (f32[1,128,2560]{1,2,0:T(8,128)}, f32[1,128,2560]{1,2,0:T(8,128)S(1)}, u32[]{:S(2)}) copy-start(f32[1,128,2560]{1,2,0:T(8,128)S(1)} %copy.255) | copy-start | bytes 3932164
  101.1 6.9 %copy-start.40 = (f32[128,128]{0,1:T(8,128)S(1)}, f32[128,128]{0,1:T(8,128)}, u32[]{:S(2)}) copy-start(f32[128,128]{0,1:T(8,128)} %copy-done.39) | copy-start | bytes 196612
  147.9 10.9 %copy-start.24 = (f32[128,40]{0,1:T(8,128)S(1)}, f32[128,40]{0,1:T(8,128)}, u32[]{:S(2)}) copy-start(f32[128,40]{0,1:T(8,128)} %get-tuple-element.312) | copy-start | bytes 61444
  158.8 4.6 %copy-start.18 = (f32[1,128,40]{1,2,0:T(8,128)S(1)}, f32[1,128,40]{1,2,0:T(8,128)}, u32[]{:S(2)}) copy-start(f32[1,128,40]{1,2,0:T(8,128)} %copy-done.17) | copy-start | bytes 61444
  158.8 4.6 %copy-start.52 = (f32[128]{0:T(128)S(1)}, f32[128]{0:T(128)}, u32[]{:S(2)}) copy-start(f32[128]{0:T(128)} %copy-done.51) | copy-start | bytes 1540
  158.8 4.6 %copy-start.58 = (f32[40]{0:T(128)S(1)}, f32[40]{0:T(128)}, u32[]{:S(2)}) copy-start(f32[40]{0:T(128)} %copy-done.57) | copy-start | bytes 484
  252.5 5.0 %copy-start.2 = (f32[128,2816]{1,0:T(8,128)S(1)}, f32[128,2816]{1,0:T(8,128)}, u32[]{:S(2)}) copy-start(f32[128,2816]{1,0:T(8,128)} %copy-done.1) | copy-start | bytes 4325380
  257.4 4.2 %copy-start.30 = (f32[2816]{0:T(1024)S(1)}, f32[2816]{0:T(1024)}, u32[]{:S(2)}) copy-start(f32[2816]{0:T(1024)} %get-tuple-element.268) | copy-start | bytes 33796
  257.4 4.2 %copy-start.32 = (f32[2816]{0:T(1024)S(1)}, f32[2816]{0:T(1024)}, u32[]{:S(2)}) copy-start(f32[2816]{0:T(1024)} %get-tuple-element.269) | copy-start | bytes 33796
  257.4 4.2 %copy-start.34 = (f32[2816]{0:T(1024)S(1)}, f32[2816]{0:T(1024)}, u32[]{:S(2)}) copy-start(f32[2816]{0:T(1024)} %get-tuple-element.270) | copy-start | bytes 33796
  257.4 4.2 %copy-start.50 = (f32[128]{0:T(128)S(1)}, f32[128]{0:T(128)}, u32[]{:S(2)}) copy-start(f32[128]{0:T(128)} %get-tuple-element.303) | copy-start | bytes 1540
  257.5 4.2 %copy-start.56 = (f32[128]{0:T(128)S(1)}, f32[128]{0:T(128)}, u32[]{:S(2)}) copy-start(f32[128]{0:T(128)} %copy-done.54) | copy-start | bytes 1540
  262.5 5.9 %copy-start.4 = (f32[1,128,2560]{1,2,0:T(8,128)S(1)}, f32[1,128,2560]{1,2,0:T(8,128)}, u32[]{:S(2)}) copy-start(f32[1,128,2560]{1,2,0:T(8,128)} %copy-done.3) | copy-start | bytes 3932164
  262.5 5.9 %copy-start.13 = (f32[128,128]{1,0:T(8,128)S(1)}, f32[128,128]{1,0:T(8,128)}, u32[]{:S(2)}) copy-start(f32[128,128]{1,0:T(8,128)} %copy-done.12) | copy-start | bytes 196612
  268.4 7.7 %copy-start.42 = (f32[2816]{0:T(1024)S(1)}, f32[2816]{0:T(1024)}, u32[]{:S(2)}) copy-start(f32[2816]{0:T(1024)} %get-tuple-element.260) | copy-start | bytes 33796
  268.4 8.6 %copy-start.53 = (f32[128]{0:T(128)S(1)}, f32[128]{0:T(128)}, u32[]{:S(2)}) copy-start(f32[128]{0:T(128)} %copy-done.51) | copy-start | bytes 1540
  271.6 7.5 %copy-start.23 = (f32[128,40]{0,1:T(8,128)S(1)}, f32[128,40]{0,1:T(8,128)}, u32[]{:S(2)}) copy-start(f32[128,40]{0,1:T(8,128)} %get-tuple-element.266) | copy-start | bytes 61444
  271.6 7.6 %copy-start.28 = (bf16[4,32,40]{2,0,1:T(4,128)(2,1)S(1)}, bf16[4,32,40]{2,0,1:T(4,128)(2,1)}, u32[]{:S(2)}) copy-start(bf16[4,32,40]{2,0,1:T(4,128)(2,1)} %copy-done.27) | copy-start | bytes 30724
  271.6 7.6 %copy-start.61 = (f32[40]{0:T(128)S(1)}, f32[40]{0:T(128)}, u32[]{:S(2)}) copy-start(f32[40]{0:T(128)} %param.20) | copy-start | bytes 484
  271.6 7.6 %copy-start.63 = (f32[40]{0:T(128)S(1)}, f32[40]{0:T(128)}, u32[]{:S(2)}) copy-start(f32[40]{0:T(128)} %param.21) | copy-start | bytes 484
  271.6 7.7 %copy-start.75 = (bf16[4]{0:T(256)(128)(2,1)S(1)}, bf16[4]{0:T(256)(128)(2,1)}, u32[]{:S(2)}) copy-start(bf16[4]{0:T(256)(128)(2,1)} %copy-done.74) | copy-start | bytes 28
  271.6 7.7 %copy-start.79 = (bf16[4]{0:T(256)(128)(2,1)S(1)}, bf16[4]{0:T(256)(128)(2,1)}, u32[]{:S(2)}) copy-start(bf16[4]{0:T(256)(128)(2,1)} %copy-done.78) | copy-start | bytes 28
  271.6 11.9 %copy-start.44 = (bf16[3,2816]{1,0:T(4,128)(2,1)S(1)}, bf16[3,2816]{1,0:T(4,128)(2,1)}, u32[]{:S(2)}) copy-start(bf16[3,2816]{1,0:T(4,128)(2,1)} %split.13) | copy-start | bytes 50692
  271.6 13.2 %copy-start.21 = (f32[128,40]{0,1:T(8,128)S(1)}, f32[128,40]{0,1:T(8,128)}, u32[]{:S(2)}) copy-start(f32[128,40]{0,1:T(8,128)} %copy-done.20) | copy-start | bytes 61444
  271.6 13.2 %copy-start.22 = (f32[128,40]{0,1:T(8,128)S(1)}, f32[128,40]{0,1:T(8,128)}, u32[]{:S(2)}) copy-start(f32[128,40]{0,1:T(8,128)} %get-tuple-element.257) | copy-start | bytes 61444
  271.6 13.2 %copy-start.35 = (f32[1,128,40]{1,2,0:T(8,128)S(1)}, f32[1,128,40]{1,2,0:T(8,128)}, u32[]{:S(2)}) copy-start(f32[1,128,40]{1,2,0:T(8,128)} %copy.297) | copy-start | bytes 61444
  271.6 13.5 %copy-start.8 = (f32[128,2816]{1,0:T(8,128)S(1)}, f32[128,2816]{1,0:T(8,128)}, u32[]{:S(2)}) copy-start(f32[128,2816]{1,0:T(8,128)} %slice_add_fusion) | copy-start | bytes 4325380
  280.3 10.7 %all-to-all-start.4 = ((bf16[4,2,640]{2,1,0:T(2,128)(2,1)}), bf16[4,2,640]{2,1,0:T(2,128)(2,1)S(1)}, u32[]{:S(2)}, u32[]{:S(2)}) async-start(bf16[4,2,640]{2,1,0:T(2,128)(2,1)} %reshape.953), calls=%async_computation.4 | async-start | bytes 20480 | tf_op jit(solution)/shard_map/all_to_all | solution.py:301
  283.5 5.7 %collective-permute-start.2 = (bf16[3,2816]{1,0:T(4,128)(2,1)S(1)}, bf16[3,2816]{1,0:T(4,128)(2,1)S(1)}, u32[]{:S(2)}, u32[]{:S(2)}) collective-permute-start(bf16[3,2816]{1,0:T(4,128)(2,1)S(1)} %copy-done.44), channel_id=1, source_target_pairs={{4,0},{8,4},{12,8},{16,12},{20,16},{24,20},{28,24},{5,1},{9,5},{13... | collective-permute-start | bytes 50696 | tf_op jit(solution)/shard_map/ppermute | solution.py:12
  290.0 4.5 %copy-start.41 = (f32[2816]{0:T(1024)S(1)}, f32[2816]{0:T(1024)}, u32[]{:S(2)}) copy-start(f32[2816]{0:T(1024)} %get-tuple-element.259) | copy-start | bytes 33796
  290.1 4.5 %copy-start.68 = (f32[40]{0:T(128)S(1)}, f32[40]{0:T(128)}, u32[]{:S(2)}) copy-start(f32[40]{0:T(128)} %reduce_sum.233) | copy-start | bytes 484
  290.1 48.6 %copy-start.77 = (s32[4]{0:T(128)S(1)}, s32[4]{0:T(128)}, u32[]{:S(2)}) copy-start(s32[4]{0:T(128)} %copy-done.76) | copy-start | bytes 52
  291.0 48.6 %all-to-all-start.3 = ((bf16[4,32,2816]{2,1,0:T(8,128)(2,1)}), bf16[4,32,2816]{2,1,0:T(8,128)(2,1)S(1)}, u32[]{:S(2)}, u32[]{:S(2)}) async-start(bf16[4,32,2816]{2,1,0:T(8,128)(2,1)} %copy.280), calls=%async_computation.3 | async-start | bytes 1441792 | tf_op jit(solution)/shard_map/all_to_all | solution.py:300
  (26 other events, 51.9 us)
Sparse Core Ops, SparseCore 0:
  60.3 87.3 all-gather.7
  149.9 84.3 all-gather.5
where the time goes:
time: 351 us; the launch traced here: 348 us
  waiting for transfers between devices  123 us (35%)
  blocking collectives  64.3 us (18%)
  other arithmetic  51.2 us (15%)
  local copies, waits for them, and re-layouts  34.5 us (10%)
  matrix products  32.4 us (9%)
  starting transfers between devices  26.5 us (8%)
  between operations  15.9 us (5%)
    all_gather x1, waiting for transfers between devices, prefix(): lax.all_gather(part.astype(kind), axis)  68.2 us
    psum x1, blocking collectives, per_device(): lax.psum((grad_weight, grad_bias, grad_step_bias, grad_rate_front + grad_...  43.9 us
    all_gather x1, waiting for transfers between devices, carried_in(): lax.all_gather(a.astype(kind), axis)  37.6 us
    dot_general x12, matrix products, contract(): return jnp.einsum(form, left, right, preferred_element_type=jnp.float32)  27.3 us
    all_gather x1, blocking collectives, prefix(): lax.all_gather(part.astype(kind), axis)  20.4 us
    select_n x8, other arithmetic, step(): return jax.tree.map(lambda a, b: jnp.where(reached, a, b), new, before)  11.3 us
    add x7, other arithmetic, join_segments(): next_decay[:, None, None] * first_state + next_state  9.99 us
    ppermute x3, starting transfers between devices, shifted(): return lax.ppermute(x, axis, pairs)  8.74 us
  transfers between devices with their start and end apart: 10, of which 6 were waited for; matrix products, arithmetic and copies ran while one was open for 18% of the time, Pallas kernels for 0%

commit v1 on v0

v1 whole, which is shorter than its diff:
```python
import functools

import jax
import jax.numpy as jnp
from jax import lax
from jax.experimental import pallas as pl
from jax.experimental.pallas import tpu as pltpu
from jax.sharding import PartitionSpec as P

F32 = jnp.float32
BF16 = jnp.bfloat16
LANES = 128
PAD = 8
WIDE = 256
LAG = 2
VMEM_LIMIT = 56 * 1024 * 1024
HIGH = lax.Precision.HIGHEST


def vmem():
    return pl.BlockSpec(memory_space=pltpu.VMEM)


def smem():
    return pl.BlockSpec(memory_space=pltpu.SMEM)


def dot(a, b, dims=((1,), (0,)), precision=None):
    return lax.dot_general(
        a, b, (dims, ((), ())), preferred_element_type=F32, precision=precision
    )


def iota(shape, dim):
    return lax.broadcasted_iota(jnp.int32, shape, dim)


def arrange_kernel(pack_ref, rows_ref, dt_ref, send_ref, tail_ref, tag_ref):
    held, block, width = send_ref.shape
    channels = rows_ref.shape[2]
    heads = dt_ref.shape[2]
    for j in range(held):
        to = pack_ref[j, 0]
        send_ref[to, :, :channels] = rows_ref[j]
        send_ref[to, :, channels:] = jnp.zeros((block, width - channels), BF16)
        send_ref[to, :, channels : channels + heads] = dt_ref[j]
        tail_ref[to] = rows_ref[j, block - 2 * PAD :, :].astype(F32)[PAD:].astype(BF16)
        tag_ref[to] = jnp.full((8, LANES), pack_ref[j, 1], jnp.int32)


def peers_barrier(seq_axis_peers, groups, me_s, me_d, n_seq):
    barrier = pltpu.get_barrier_semaphore()

    def tell(s, d):
        pl.semaphore_signal(
            barrier, inc=1, device_id={"seq": s, "dp": d}, device_id_type=pl.DeviceIdType.MESH
        )

    for k in range(1, groups):
        tell(me_s, lax.rem(me_d + k, groups))
    for step in (1, -1):
        ok = (me_s + step >= 0) & (me_s + step < n_seq)

        @pl.when(ok)
        def _():
            for d in range(groups if seq_axis_peers == "all" else 0):
                tell(me_s + step, d)

    pl.semaphore_wait(barrier, groups - 1 + groups * sides(me_s, n_seq))


def sides(me, count):
    return (me > 0).astype(jnp.int32) + (me < count - 1).astype(jnp.int32)


def remote(src, dst, ssem, rsem, s, d):
    return pltpu.make_async_remote_copy(
        src_ref=src,
        dst_ref=dst,
        send_sem=ssem,
        recv_sem=rsem,
        device_id={"seq": s, "dp": d},
        device_id_type=pl.DeviceIdType.MESH,
    )


def spread_kernel(
    n_seq, groups,
    send_ref, tail_ref, tag_ref, reset_ref,
    got_ref, gtag_ref, ptail_ref, ptag_ref, preset_ref,
    ss, rs, tss, trs, qss, qrs, uss, urs, wss, wrs, lsem,
):
    me_s, me_d = lax.axis_index("seq"), lax.axis_index("dp")
    peers_barrier("all", groups, me_s, me_d, n_seq)
    row_copies = []
    for k in range(1, groups):
        d = lax.rem(me_d + k, groups)
        a = remote(send_ref.at[d], got_ref.at[me_d], ss.at[k], rs.at[k], me_s, d)
        b = remote(tag_ref.at[d], gtag_ref.at[me_d], tss.at[k], trs.at[k], me_s, d)
        a.start()
        b.start()
        row_copies += [a, b]
    own = [
        pltpu.make_async_copy(send_ref.at[me_d], got_ref.at[me_d], lsem.at[0]),
        pltpu.make_async_copy(tag_ref.at[me_d], gtag_ref.at[me_d], lsem.at[1]),
    ]
    for c in own:
        c.start()

    def tails():
        out = []
        for k in range(groups):
            d = lax.rem(me_d + k, groups)
            out.append(remote(tail_ref.at[d], ptail_ref.at[me_d], qss.at[k], qrs.at[k], me_s + 1, d))
            out.append(remote(tag_ref.at[d], ptag_ref.at[me_d], uss.at[k], urs.at[k], me_s + 1, d))
        out.append(remote(reset_ref, preset_ref, wss, wrs, me_s + 1, me_d))
        return out

    @pl.when(me_s + 1 < n_seq)
    def _():
        for c in tails():
            c.start()

    @pl.when(me_s == 0)
    def _():
        ptail_ref[...] = jnp.zeros(ptail_ref.shape, BF16)
        ptag_ref[...] = jnp.zeros(ptag_ref.shape, jnp.int32)
        preset_ref[...] = jnp.zeros(preset_ref.shape, jnp.int32)

    for c in own:
        c.wait()
    for c in row_copies:
        c.wait()

    @pl.when(me_s + 1 < n_seq)
    def _():
        for c in tails():
            c.wait_send()

    @pl.when(me_s > 0)
    def _():
        for c in tails():
            c.wait_recv()


def token_values(dtp, bias_row, rate_row, reset_row):
    length = dtp.shape[0]
    t_i = iota((length, length), 0)
    s_i = iota((length, length), 1)
    raw = dtp + bias_row
    size = jnp.maximum(raw, 0.0) + jnp.log1p(jnp.exp(-jnp.abs(raw)))
    log_decay = -size * rate_row
    lower = (t_i >= s_i).astype(F32)
    cum = dot(lower, log_decay, precision=HIGH)
    cum_t = dot(log_decay, lower, ((0,), (1,)), precision=HIGH)
    flags = jnp.broadcast_to(reset_row.astype(F32), (length, length))
    seg_col = jnp.sum(jnp.where(t_i >= s_i, flags, 0.0), axis=1, keepdims=True)
    reset_col = jnp.sum(jnp.where(t_i == s_i, flags, 0.0), axis=1, keepdims=True)
    seg_row = jnp.sum(
        jnp.where(t_i <= s_i, jnp.broadcast_to(reset_col, (length, length)), 0.0),
        axis=0, keepdims=True,
    )
    last = cum[length - 1 : length, :]
    seg_last = seg_col[length - 1 : length, :]
    weight = jnp.where(seg_col == seg_last, jnp.exp(last - cum), 0.0)
    entry = jnp.where(seg_col == 0.0, jnp.exp(cum), 0.0)
    decay = jnp.where(seg_last == 0.0, jnp.exp(last), 0.0)
    allowed = (t_i >= s_i) & (seg_col == seg_row)
    return raw, size, cum, cum_t, weight, entry, decay, allowed, reset_col


def pair(x, i, head_size, rows):
    per = LANES // head_size
    lane = iota((rows, LANES), 1) // head_size
    out = jnp.broadcast_to(x[:, per * i : per * i + 1], (rows, LANES))
    for k in range(1, per):
        out = jnp.where(lane == k, x[:, per * i + k : per * i + k + 1], out)
    return out


def front_kernel(
    inner, head_size, n_state,
    tag_ref, ptag_ref,
    got_ref, ptail_ref, reset_ref, preset_ref, weight_ref, cbias_ref, sbias_ref, rate_ref, gout_ref,
    ext_ref, act_ref, slope_ref, dtp_ref, join_ref, state_ref, gstate_ref, decay_ref,
):
    groups, block, width = got_ref.shape
    length = act_ref.shape[0]
    channels = act_ref.shape[1]
    held = length // block
    for g in range(groups):
        slot = tag_ref[g, 0, 0] - 0
        start = pl.multiple_of(slot * block, block)
        ext_ref[pl.ds(start + PAD, block), :] = got_ref[g, :, :channels].astype(F32)
        dtp_ref[pl.ds(start, block), :] = got_ref[g, :, channels:].astype(F32)
    prior = jnp.zeros((PAD, channels), F32)
    for g in range(groups):
        prior = jnp.where(ptag_ref[g, 0, 0] == held - 1, ptail_ref[g].astype(F32), prior)
    ext_ref[0:PAD, :] = prior

    raw, size, cum, cum_t, wgt, ent, dec, allowed, reset_col = token_values(
        dtp_ref[...], sbias_ref[...], rate_ref[...], reset_ref[...]
    )
    prev = jnp.broadcast_to(preset_ref[...].astype(F32), (PAD, length))
    pick = iota((PAD, length), 1) == iota((PAD, length), 0) + (length - PAD)
    prev_col = jnp.sum(jnp.where(pick, prev, 0.0), axis=1, keepdims=True)
    flags = jnp.concatenate([prev_col, reset_col], axis=0)
    flags = jnp.broadcast_to(flags, (length + PAD, LANES))
    keep = 1.0 - flags
    j1 = keep[PAD:]
    j2 = j1 * keep[PAD - 1 : PAD - 1 + length]
    j3 = j2 * keep[PAD - 2 : PAD - 2 + length]
    join_ref[0] = j1
    join_ref[1] = j2
    join_ref[2] = j3
    for lo in range(0, channels, LANES):
        sl = slice(lo, lo + LANES)
        v = cbias_ref[:, sl] + weight_ref[3:4, sl] * ext_ref[PAD:, sl]
        v = v + weight_ref[2:3, sl] * (ext_ref[PAD - 1 : PAD - 1 + length, sl] * j1)
        v = v + weight_ref[1:2, sl] * (ext_ref[PAD - 2 : PAD - 2 + length, sl] * j2)
        v = v + weight_ref[0:1, sl] * (ext_ref[PAD - 3 : PAD - 3 + length, sl] * j3)
        sig = jax.nn.sigmoid(v)
        act_ref[:, sl] = (v * sig).astype(BF16)
        slope_ref[:, sl] = sig * (1.0 + v * (1.0 - sig))
    b_rows = act_ref[:, inner : inner + n_state]
    c_rows = act_ref[:, inner + n_state :]
    for i in range(inner // LANES):
        sl = slice(i * LANES, (i + 1) * LANES)
        at, lo = divmod(i * LANES, WIDE)
        xs = (act_ref[:, sl].astype(F32) * pair(size, i, head_size, length)).astype(BF16)
        xw = (xs.astype(F32) * pair(wgt, i, head_size, length)).astype(BF16)
        ed = (gout_ref[:, sl].astype(F32) * pair(ent, i, head_size, length)).astype(BF16)
        state_ref[at, :, lo : lo + LANES] = dot(b_rows, xw, ((0,), (0,))).astype(BF16)
        gstate_ref[at, :, lo : lo + LANES] = dot(c_rows, ed, ((0,), (0,))).astype(BF16)
        decay_ref[at, :, lo : lo + LANES] = pair(jnp.broadcast_to(dec, (8, LANES)), i, head_size, 8)


def chain_kernel(
    n_seq, state_ref, gstate_ref, decay_ref, enter_ref, after_ref,
    fout, bout, fin, bin_, fss, frs, bss, brs,
):
    me, me_d = lax.axis_index("seq"), lax.axis_index("dp")
    pieces = state_ref.shape[0]
    barrier = pltpu.get_barrier_semaphore()
    for step in (1, -1):
        ok = (me + step >= 0) & (me + step < n_seq)

        @pl.when(ok)
        def _():
            pl.semaphore_signal(
                barrier, inc=1, device_id={"seq": me + step, "dp": me_d},
                device_id_type=pl.DeviceIdType.MESH,
            )

    pl.semaphore_wait(barrier, sides(me, n_seq))

    def one(c, first, final, local, got, out, result, ssem, rsem, to):
        copy = remote(out.at[c], got.at[c], ssem.at[c], rsem.at[c], to, me_d)

        @pl.when(first)
        def _():
            got[c] = jnp.zeros(got.shape[1:], BF16)

        @pl.when(jnp.logical_not(first))
        def _():
            copy.wait_recv()

        result[c] = got[c]

        @pl.when(jnp.logical_not(final))
        def _():
            out[c] = (decay_ref[c, 0:1, :] * got[c].astype(F32) + local[c].astype(F32)).astype(BF16)
            copy.start()

    def body(v, carry):
        cf = v - LAG * me
        cb = v - LAG * (n_seq - 1 - me)

        @pl.when((cf >= 0) & (cf < pieces))
        def _():
            one(cf, me == 0, me == n_seq - 1, state_ref, fin, fout, enter_ref, fss, frs, me + 1)

        @pl.when((cb >= 0) & (cb < pieces))
        def _():
            one(cb, me == n_seq - 1, me == 0, gstate_ref, bin_, bout, after_ref, bss, brs, me - 1)

        return carry

    lax.fori_loop(0, LAG * (n_seq - 1) + pieces, body, 0)

    def drain(c, carry):
        @pl.when(me < n_seq - 1)
        def _():
            remote(fout.at[c], fin.at[c], fss.at[c], frs.at[c], me + 1, me_d).wait_send()

        @pl.when(me > 0)
        def _():
            remote(bout.at[c], bin_.at[c], bss.at[c], brs.at[c], me - 1, me_d).wait_send()

        return carry

    lax.fori_loop(0, pieces, drain, 0)


def split_dot(a, b, dims=((1,), (0,))):
    hi = a.astype(BF16)
    lo = (a - hi.astype(F32)).astype(BF16)
    return dot(hi, b, dims) + dot(lo, b, dims)


def back_kernel(
    inner, head_size, n_state, heads, share,
    tag_ref,
    ext_ref, act_ref, slope_ref, dtp_ref, join_ref, enter_ref, after_ref,
    reset_ref, weight_ref, sbias_ref, rate_ref, gain_ref, gout_ref,
    out_ref, back_ref, spill_ref, param_ref,
    dv_ref, p_ref, grad_ref, gdt_ref, dcum_ref, dsize_ref, tot_ref,
):
    length, channels = act_ref.shape
    groups, block, _ = back_ref.shape
    per = LANES // head_size
    raw, size, cum, cum_t, wgt, ent, dec, allowed, _ = token_values(
        dtp_ref[...], sbias_ref[...], rate_ref[...], reset_ref[...]
    )
    gain = gain_ref[...]
    b_rows = act_ref[:, inner : inner + n_state]
    c_rows = act_ref[:, inner + n_state :]
    scores = dot(c_rows, b_rows, ((1,), (1,)))
    dcum_ref[...] = jnp.zeros((length, LANES), F32)
    dsize_ref[...] = jnp.zeros((length, LANES), F32)
    tot_ref[...] = jnp.zeros((16, LANES), F32)
    dscore = jnp.zeros((length, length), F32)
    db = jnp.zeros((length, n_state), F32)
    dc = jnp.zeros((length, n_state), F32)
    lane = iota((length, LANES), 1) // head_size
    row_head = iota((LANES, LANES), 0) // head_size
    col_head = iota((LANES, LANES), 1)
    dec8 = jnp.broadcast_to(dec, (8, LANES))
    gain8 = jnp.broadcast_to(gain, (8, LANES))
    for i in range(inner // LANES):
        sl = slice(i * LANES, (i + 1) * LANES)
        at, lo = divmod(i * LANES, WIDE)
        enter = enter_ref[at, :, lo : lo + LANES]
        after = after_ref[at, :, lo : lo + LANES]
        x = act_ref[:, sl].astype(F32)
        do = gout_ref[:, sl]
        do32 = do.astype(F32)
        size_b = pair(size, i, head_size, length)
        wgt_b = pair(wgt, i, head_size, length)
        ent_b = pair(ent, i, head_size, length)
        gain_b = pair(gain8, i, head_size, 8)[0:1]
        dec_b = pair(dec8, i, head_size, 8)[0:1]
        xs = (x * size_b).astype(BF16)
        xs32 = xs.astype(F32)
        within = jnp.zeros((length, LANES), F32)
        dxs = jnp.zeros((length, LANES), F32)
        for k in range(per):
            h = per * i + k
            expo = cum[:, h : h + 1] - cum_t[h : h + 1, :]
            decay = jnp.exp(jnp.where(allowed, expo, -1e30))
            mixing = (scores * decay).astype(BF16)
            mine = lane == k
            within = jnp.where(mine, dot(mixing, xs), within)
            dxs = jnp.where(mine, dot(mixing, do, ((0,), (0,))), dxs)
            dmix = dot(jnp.where(mine, do32, 0.0).astype(BF16), xs, ((1,), (1,)))
            dscore = dscore + dmix * decay
        y = within + ent_b * dot(c_rows, enter)
        out_ref[:, sl] = (y + gain_b * x).astype(BF16)
        ba = wgt_b * dot(b_rows, after)
        dxs = dxs + ba
        dv_ref[:, sl] = (dxs * size_b + gain_b * do32) * slope_ref[:, sl]
        xw = (xs32 * wgt_b).astype(BF16)
        ed = (do32 * ent_b).astype(BF16)
        db = db + dot(xw, after, ((1,), (1,)))
        dc = dc + dot(ed, enter, ((1,), (1,)))
        ind = (row_head + per * i == col_head).astype(BF16)
        dcum_ref[...] += split_dot(do32 * y - xs32 * dxs, ind)
        dsize_ref[...] += split_dot(dxs * x, ind)
        t3 = jnp.sum(xs32 * ba, axis=0, keepdims=True) + dec_b * jnp.sum(
            after.astype(F32) * enter.astype(F32), axis=0, keepdims=True
        )
        t5 = jnp.sum(do32 * x, axis=0, keepdims=True)
        both = jnp.concatenate(
            [jnp.broadcast_to(t3, (8, LANES)), jnp.broadcast_to(t5, (8, LANES))], axis=0
        )
        tot_ref[...] += split_dot(both, ind)
    dscore = dscore.astype(BF16)
    dc = dc + dot(dscore, b_rows)
    db = db + dot(dscore, c_rows, ((0,), (0,)))
    slb = slice(inner, inner + n_state)
    slc = slice(inner + n_state, channels)
    dv_ref[:, slb] = db * slope_ref[:, slb]
    dv_ref[:, slc] = dc * slope_ref[:, slc]

    t_i = iota((length, length), 0)
    s_i = iota((length, length), 1)
    is_last = iota((length, LANES), 0) == length - 1
    dcum = dcum_ref[...] + jnp.where(is_last, tot_ref[0:1, :], 0.0)
    dlog = dot((s_i >= t_i).astype(F32), dcum, precision=HIGH)
    dsize = dsize_ref[...] - dlog * rate_ref[...]
    draw = dsize * jax.nn.sigmoid(raw)
    gdt_ref[...] = draw
    param_ref[...] = jnp.zeros(param_ref.shape, F32)
    param_ref[0, 5:6, 0:LANES] = jnp.sum(draw, axis=0, keepdims=True)
    param_ref[0, 6:7, 0:LANES] = -jnp.sum(dlog * size, axis=0, keepdims=True)
    param_ref[0, 7:8, 0:LANES] = tot_ref[8:9, :]

    p_ref[:, 0:PAD, :] = jnp.zeros((3, PAD, LANES), F32)
    p_ref[:, PAD + length :, :] = jnp.zeros((3, PAD, LANES), F32)
    zeros = jnp.zeros((PAD, LANES), F32)
    for lo in range(0, channels, LANES):
        sl = slice(lo, lo + LANES)
        at, off = divmod(lo, share)
        col = slice(off, off + LANES)
        dv = dv_ref[:, sl]
        total = jnp.concatenate([zeros, weight_ref[3:4, sl] * dv], axis=0)
        param_ref[at, 3:4, col] = jnp.sum(dv * ext_ref[PAD:, sl], axis=0, keepdims=True)
        param_ref[at, 4:5, col] = jnp.sum(dv, axis=0, keepdims=True)
        for k in range(1, 4):
            pk = dv * join_ref[k - 1]
            p_ref[k - 1, PAD : PAD + length, :] = pk
            param_ref[at, 3 - k : 4 - k, col] = jnp.sum(
                pk * ext_ref[PAD - k : PAD - k + length, sl], axis=0, keepdims=True
            )
            total = total + weight_ref[3 - k : 4 - k, sl] * p_ref[k - 1, k : k + length + PAD, :]
        spill_ref[:, sl] = total[0:PAD].astype(BF16)
        grad_ref[:, sl] = total[PAD:]
    for g in range(groups):
        start = pl.multiple_of(tag_ref[g, 0, 0] * block, block)
        back_ref[g, :, :channels] = grad_ref[pl.ds(start, block), :].astype(BF16)
        back_ref[g, :, channels:] = gdt_ref[pl.ds(start, block), :].astype(BF16)


def return_kernel(
    n_seq, groups,
    back_ref, spill_ref, param_ref,
    ret_ref, rspill_ref, total_ref,
    part, mid, fin,
    ss, rs, qss, qrs, ass, ars, bss, brs, css, crs, lsem,
):
    me_s, me_d = lax.axis_index("seq"), lax.axis_index("dp")
    barrier = pltpu.get_barrier_semaphore()

    def tell(s, d):
        pl.semaphore_signal(
            barrier, inc=1, device_id={"seq": s, "dp": d}, device_id_type=pl.DeviceIdType.MESH
        )

    for k in range(1, groups):
        tell(me_s, lax.rem(me_d + k, groups))
    for k in range(1, n_seq):
        tell(lax.rem(me_s + k, n_seq), me_d)
    for step in (1, -1):
        ok = (me_s + step >= 0) & (me_s + step < n_seq)

        @pl.when(ok)
        def _():
            for k in range(1, groups):
                tell(me_s + step, lax.rem(me_d + k, groups))

    pl.semaphore_wait(barrier, groups + n_seq - 2 + (groups - 1) * sides(me_s, n_seq))

    scatter = []
    for k in range(1, n_seq):
        s = lax.rem(me_s + k, n_seq)
        scatter.append(remote(param_ref.at[s], part.at[k], ass.at[k], ars.at[k], s, me_d))
    for c in scatter:
        c.start()
    rows = []
    for k in range(1, groups):
        d = lax.rem(me_d + k, groups)
        rows.append(remote(back_ref.at[d], ret_ref.at[me_d], ss.at[k], rs.at[k], me_s, d))
    for c in rows:
        c.start()
    own = pltpu.make_async_copy(back_ref.at[me_d], ret_ref.at[me_d], lsem)
    own.start()

    def spills():
        return [
            remote(
                spill_ref, rspill_ref.at[me_d], qss.at[k], qrs.at[k], me_s - 1,
                lax.rem(me_d + k, groups),
            )
            for k in range(groups)
        ]

    @pl.when(me_s > 0)
    def _():
        for c in spills():
            c.start()

    @pl.when(me_s == n_seq - 1)
    def _():
        rspill_ref[...] = jnp.zeros(rspill_ref.shape, BF16)

    for c in scatter:
        c.wait()
    mine = param_ref[me_s]
    for k in range(1, n_seq):
        mine = mine + part[k]
    mid[0] = mine
    across = [
        remote(mid.at[0], mid.at[k], bss.at[k], brs.at[k], me_s, lax.rem(me_d + k, groups))
        for k in range(1, groups)
    ]
    for c in across:
        c.start()
    for c in across:
        c.wait()
    total = jnp.zeros(mine.shape, F32)
    for d in range(groups):
        total = total + mid[lax.rem(me_d - d + groups, groups)]
    fin[...] = total
    total_ref[me_s] = total
    gather = [
        remote(fin, total_ref.at[me_s], css.at[k], crs.at[k], lax.rem(me_s + k, n_seq), me_d)
        for k in range(1, n_seq)
    ]
    for c in gather:
        c.start()
    for c in rows:
        c.wait()
    own.wait()

    @pl.when(me_s > 0)
    def _():
        for c in spills():
            c.wait_send()

    @pl.when(me_s < n_seq - 1)
    def _():
        for c in spills():
            c.wait_recv()

    for c in gather:
        c.wait()


def place_kernel(
    share, pack_ref, ret_ref, rspill_ref, total_ref,
    gin_ref, gdt_ref, gw_ref, gb_ref, gsb_ref, grate_ref, ggain_ref,
):
    held, block, channels = gin_ref.shape
    heads = gdt_ref.shape[2]
    for j in range(held):
        g = pack_ref[j, 0]
        gin_ref[j] = ret_ref[g, :, :channels]
        gdt_ref[j] = ret_ref[g, :, channels : channels + heads]
        low = ret_ref[g, block - 2 * PAD :, :channels].astype(F32)
        extra = rspill_ref[g].astype(F32)
        last = pack_ref[j, 1] == held - 1
        extra = jnp.where(last, extra, 0.0)
        gin_ref[j, block - 2 * PAD :, :] = jnp.concatenate(
            [low[:PAD], low[PAD:] + extra], axis=0
        ).astype(BF16)
    for lo in range(0, channels, LANES):
        at, off = divmod(lo, share)
        gw_ref[:, lo : lo + LANES] = total_ref[at, 0:4, off : off + LANES]
        gb_ref[:, lo : lo + LANES] = total_ref[at, 4:5, off : off + LANES]
    gsb_ref[...] = total_ref[0, 5:6, 0:heads]
    grate_ref[...] = total_ref[0, 6:7, 0:heads]
    ggain_ref[...] = total_ref[0, 7:8, 0:heads]


def shape(dims, kind):
    return jax.ShapeDtypeStruct(dims, kind)


def call(kernel, ins, outs, scratch=(), cid=None):
    extra = {} if cid is None else {"collective_id": cid, "has_side_effects": True}
    return pl.pallas_call(
        kernel,
        out_shape=outs,
        in_specs=ins,
        out_specs=tuple(vmem() for _ in outs),
        scratch_shapes=list(scratch),
        compiler_params=pltpu.CompilerParams(vmem_limit_bytes=VMEM_LIMIT, **extra),
    )


def per_device(
    conv_input, dt_raw, packing, resets, conv_weight, conv_bias, dt_bias, decay_rate, skip_gain, grad_out
):
    groups = lax.axis_size("dp")
    n_seq = lax.axis_size("seq")
    length, channels = conv_input.shape[1:]
    heads = dt_raw.shape[2]
    inner = grad_out.shape[2]
    head_size = inner // heads
    n_state = (channels - inner) // 2
    held = packing.shape[1]
    block = length // held
    width = channels + LANES
    pack = packing[0]
    dma = pltpu.SemaphoreType.DMA
    row = lambda a: a.reshape(1, -1)
    padded = lambda a: jnp.pad(row(a), ((0, 0), (0, LANES - heads)))

    send, tail, tag = call(
        arrange_kernel,
        [smem(), vmem(), vmem()],
        (
            shape((groups, block, width), BF16),
            shape((groups, PAD, channels), BF16),
            shape((groups, 8, LANES), jnp.int32),
        ),
    )(pack, conv_input[0].reshape(held, block, channels), dt_raw[0].reshape(held, block, heads))

    got, gtag, ptail, ptag, preset = call(
        functools.partial(spread_kernel, n_seq, groups),
        [vmem()] * 4,
        (
            shape((groups, block, width), BF16),
            shape((groups, 8, LANES), jnp.int32),
            shape((groups, PAD, channels), BF16),
            shape((groups, 8, LANES), jnp.int32),
            shape((1, length), jnp.int32),
        ),
        [dma((groups,))] * 8 + [dma, dma, dma((2,))],
        cid=0,
    )(send, tail, tag, resets)

    sbias, rate, gain = padded(dt_bias), padded(decay_rate), padded(skip_gain)
    pieces = inner // WIDE
    state_shape = shape((pieces, n_state, WIDE), BF16)
    ext, act, slope, dtp, join, state, gstate, decay = call(
        functools.partial(front_kernel, inner, head_size, n_state),
        [smem(), smem()] + [vmem()] * 9,
        (
            shape((length + PAD, channels), F32),
            shape((length, channels), BF16),
            shape((length, channels), F32),
            shape((length, LANES), F32),
            shape((3, length, LANES), F32),
            state_shape,
            state_shape,
            shape((pieces, 8, WIDE), F32),
        ),
    )(
        gtag[:, :1, :1], ptag[:, :1, :1], got, ptail, resets, preset, conv_weight, row(conv_bias),
        sbias, rate, grad_out[0],
    )

    enter, after = call(
        functools.partial(chain_kernel, n_seq),
        [vmem()] * 3,
        (state_shape, state_shape),
        [pltpu.VMEM(state_shape.shape, BF16)] * 4 + [dma((pieces,))] * 4,
        cid=1,
    )(state, gstate, decay)

    tiles = channels // LANES
    share = -(-tiles // n_seq) * LANES
    params = shape((n_seq, 8, share), F32)
    out, back, spill, param = call(
        functools.partial(back_kernel, inner, head_size, n_state, heads, share),
        [smem()] + [vmem()] * 13,
        (
            shape((length, inner), BF16),
            shape((groups, block, width), BF16),
            shape((PAD, channels), BF16),
            params,
        ),
        [
            pltpu.VMEM((length, channels), F32),
            pltpu.VMEM((3, length + 2 * PAD, LANES), F32),
            pltpu.VMEM((length, channels), F32),
            pltpu.VMEM((length, LANES), F32),
            pltpu.VMEM((length, LANES), F32),
            pltpu.VMEM((length, LANES), F32),
            pltpu.VMEM((16, LANES), F32),
        ],
    )(
        gtag[:, :1, :1], ext, act, slope, dtp, join, enter, after, resets, conv_weight, sbias, rate,
        gain, grad_out[0],
    )

    ret, rspill, total = call(
        functools.partial(return_kernel, n_seq, groups),
        [vmem()] * 3,
        (
            shape((groups, block, width), BF16),
            shape((groups, PAD, channels), BF16),
            params,
        ),
        [
            pltpu.VMEM((n_seq, 8, share), F32),
            pltpu.VMEM((groups, 8, share), F32),
            pltpu.VMEM((8, share), F32),
        ]
        + [dma((groups,))] * 4
        + [dma((n_seq,))] * 2
        + [dma((groups,))] * 2
        + [dma((n_seq,))] * 2
        + [dma],
        cid=2,
    )(back, spill, param)

    gin, gdt, gw, gb, gsb, grate, ggain = call(
        functools.partial(place_kernel, share),
        [smem()] + [vmem()] * 3,
        (
            shape((held, block, channels), BF16),
            shape((held, block, heads), BF16),
            shape((4, channels), F32),
            shape((1, channels), F32),
            shape((1, heads), F32),
            shape((1, heads), F32),
            shape((1, heads), F32),
        ),
    )(pack, ret, rspill, total)
    return (
        out[None],
        gin.reshape(1, length, channels),
        gdt.reshape(1, length, heads),
        gw,
        gb[0],
        gsb[0],
        grate[0],
        ggain[0],
    )


def solution(mesh):
    tokens = P("dp", "seq", None)
    in_specs = (tokens, tokens, tokens, P("dp", "seq"), P(), P(), P(), P(), P(), tokens)
    out_specs = (tokens, tokens, tokens, P(), P(), P(), P(), P())
    return jax.shard_map(
        per_device, mesh=mesh, in_specs=in_specs, out_specs=out_specs, check_vma=False
    )
```

time: 351 us -> 130 us (0.37)
  waiting for transfers between devices: 123 us -> 0 us
  Pallas kernels: 0 us -> 116 us
  blocking collectives: 64.3 us -> 0 us
  other arithmetic: 51.2 us -> 1.33 us
  matrix products: 32.4 us -> 0 us
  starting transfers between devices: 26.5 us -> 0 us
  local copies, waits for them, and re-layouts: 34.5 us -> 11.6 us
  between operations: 15.9 us -> 0.66 us
    pallas_call x0 -> x7, Pallas kernels: none -> 116 us  [the longest x1 56.2 us: per_device(): call(functools.partial(chain_kernel, n_seq), [vmem()] * 3, (state_shape,...]
    all_gather x2 -> x0, waiting for transfers between devices: 106 us -> none  [the longest x1 68.2 us: prefix(): lax.all_gather(part.astype(kind), axis)]
    psum x1 -> x0, blocking collectives: 43.9 us -> none  [per_device(): lax.psum((grad_weight, grad_bias, grad_step_bias, grad_rate_front + grad_...]
    dot_general x21 -> x0, matrix products: 32.4 us -> none  [the longest x12 27.3 us: contract(): return jnp.einsum(form, left, right, preferred_element_type=jnp.float32)]
    all_gather x1 -> x0, blocking collectives: 20.4 us -> none  [prefix(): lax.all_gather(part.astype(kind), axis)]
    all_to_all x5 -> x0, starting transfers between devices: 17.7 us -> none  [the longest x1 4.21 us: per_device(): lax.all_to_all(send_tag, 'dp', split_axis=0, concat_axis=0, tiled=True)]
    all_to_all x5 -> x0, waiting for transfers between devices: 11.8 us -> none  [the longest x1 8.69 us: per_device(): lax.all_to_all(send_rows, 'dp', split_axis=0, concat_axis=0, tiled=True)]
    select_n x9 -> x0, other arithmetic: 11.4 us -> none  [the longest x8 11.3 us: step(): return jax.tree.map(lambda a, b: jnp.where(reached, a, b), new, before)]
  transfers between devices with their start and end apart: 10 -> 0, of which waited for: 6 -> 0; matrix products, arithmetic and copies ran while one was open for 18% -> 0% of each run, Pallas kernels for 0% -> 0%
where the time goes in v1:
time: 130 us
  Pallas kernels  116 us (89%)
  local copies, waits for them, and re-layouts  11.6 us (9%)
  other arithmetic  1.33 us (1%)
    pallas_call x1, Pallas kernels, per_device(): call(functools.partial(chain_kernel, n_seq), [vmem()] * 3, (state_shape,...  56.2 us
    pallas_call x1, Pallas kernels, per_device(): call(functools.partial(return_kernel, n_seq, groups), [vmem()] * 3, (shap...  19.2 us
    pallas_call x1, Pallas kernels, per_device(): call(functools.partial(spread_kernel, n_seq, groups), [vmem()] * 4, (shap...  17.3 us
    pallas_call x1, Pallas kernels, per_device(): call(functools.partial(back_kernel, inner, head_size, n_state, heads, sha...  12.6 us
    pallas_call x1, Pallas kernels, per_device(): call(functools.partial(front_kernel, inner, head_size, n_state), [smem(),...  6.53 us
    pad x3, local copies, waits for them, and re-layouts, per_device(): padded = lambda a: jnp.pad(row(a), ((0, 0), (0, LANES - heads)))  3.51 us
    unnamed x2, local copies, waits for them, and re-layouts  2.85 us

profile of v1, /device:TPU:0, one launch (start us, length us, event | category | flops | bytes accessed | tf_op | source)
XLA Modules:
  0.0 129.7 jit_solution(15118889200182887315)
XLA Ops:
  0.6 1.2 pad.10.sbias_ref
  1.8 1.2 pad.11.rate_ref
  3.0 1.2 pad.12.gain_ref
  4.1 1.3 %copy.19.pack_ref = s32[4,2]{1,0:T(4,128)} copy(s32[4,2]{0,1:T(2,128)} %bitcast.18) | data formatting | bytes 64 | tf_op jit(solution)/shard_map/squeeze | solution.py:594
  5.5 1.3 %reshape.34.cbias_ref = f32[1,2816]{1,0:T(1,128)} reshape(f32[2816]{0:T(1024)} %param.15) | data formatting | bytes 22528 | tf_op jit(solution)/shard_map/reshape | solution.py:596
  6.8 1.4 %copy.18 = bf16[1,128,40]{2,1,0:T(8,128)(2,1)} copy(bf16[1,128,40]{1,2,0:T(8,128)(2,1)} %param.11) | data formatting | bytes 20480 | tf_op args[1]
  8.2 2.1 %shard_map.161 = (bf16[4,32,2944]{2,1,0:T(8,128)(2,1)}, bf16[4,8,2816]{2,1,0:T(8,128)(2,1)}, s32[4,8,128]{2,1,0:T(8,128)}) custom-call(s32[4,2]{1,0:T(4,128)} %copy.19.pack_ref, bf16[4,32,2816]{2,1,0:T(8,128)(2,1)} %bitcast.15, bf16[4,32,40]{2,1,0:T(8,128)(2,1)} %bitcast.16), custom_call_target="tpu_custom_call" | custom-call | tf_op jit(solution)/shard_map/pallas_call | solution.py:599
  10.3 17.3 %shard_map.162 = (bf16[4,32,2944]{2,1,0:T(8,128)(2,1)}, s32[4,8,128]{2,1,0:T(8,128)}, bf16[4,8,2816]{2,1,0:T(8,128)(2,1)}, s32[4,8,128]{2,1,0:T(8,128)}, s32[1,128]{1,0:T(1,128)}) custom-call(bf16[4,32,2944]{2,1,0:T(8,128)(2,1)} %get-tuple-element.40.send_ref, bf16[4,8,2816]{2,1,0:T(8,128)(2,1)} %get-tuple-element.41.tail_ref, ...), custom_call_target="tpu_custom_call" | custom-call | tf_op jit(solution)/shard_map/pallas_call | solution.py:609
  27.6 1.3 %slice.7.tag_ref = s32[4,1,1]{2,1,0:T(1,128)} slice(s32[4,8,128]{2,1,0:T(8,128)} %get-tuple-element.43), slice={[0:4], [0:1], [0:1]} | slice | bytes 32 | tf_op jit(solution)/shard_map/slice | solution.py:674
  29.0 1.3 slice.8.ptag_ref
  30.3 6.5 %shard_map.163 = (f32[136,2816]{1,0:T(8,128)}, bf16[128,2816]{1,0:T(8,128)(2,1)}, f32[128,2816]{1,0:T(8,128)}, f32[128,128]{1,0:T(8,128)}, f32[3,128,128]{2,1,0:...) custom-call(s32[4,1,1]{2,1,0:T(1,128)} %slice.7.tag_ref, ...), custom_call_target="tpu_custom_call" | custom-call | tf_op jit(solution)/shard_map/pallas_call | solution.py:626
  36.8 56.2 %shard_map.164 = (bf16[10,128,256]{2,1,0:T(8,128)(2,1)}, bf16[10,128,256]{2,1,0:T(8,128)(2,1)}) custom-call(bf16[10,128,256]{2,1,0:T(8,128)(2,1)} %get-tuple-element.53.state_ref, bf16[10,128,256]{2,1,0:T(8,128)(2,1)} %get-tuple-element.54.gstate_ref, f32[10,8,256]{2,1,0:T(8,128)} %get-tuple-element.55.decay_ref), custom_call_target="tpu_custom_call" | custom-call | tf_op jit(solution)/shard_map/pallas_call | solution.py:644
  92.9 12.6 %shard_map.165 = (bf16[128,2560]{1,0:T(8,128)(2,1)}, bf16[4,32,2944]{2,1,0:T(8,128)(2,1)}, bf16[8,2816]{1,0:T(8,128)(2,1)}, f32[8,8,384]{2,1,0:T(8,128)}) custom-call(s32[4,1,1]{2,1,0:T(1,128)} %slice.7.tag_ref, f32[136,2816]{1,0:T(8,128)} %get-tuple-element.48.ext_ref, bf16[128,2816]{1,0:T(8,128)(2,1)} %get-tuple-element.49.act_ref, ...), custom_call_target="tpu_custom_call" | custom-call | tf_op jit(solution)/shard_map/pallas_call | solution.py:655
  105.5 19.2 %shard_map.166 = (bf16[4,32,2944]{2,1,0:T(8,128)(2,1)}, bf16[4,8,2816]{2,1,0:T(8,128)(2,1)}, f32[8,8,384]{2,1,0:T(8,128)}) custom-call(bf16[4,32,2944]{2,1,0:T(8,128)(2,1)} %get-tuple-element.59.back_ref, bf16[8,2816]{1,0:T(8,128)(2,1)} %get-tuple-element.60.spill_ref, f32[8,8,384]{2,1,0:T(8,128)} %get-tuple-element.61.param_ref), custom_call_target="tpu_custom_call" | custom-call | tf_op jit(solution)/shard_map/pallas_call | solution.py:678
  124.7 2.2 %shard_map.167 = (bf16[4,32,2816]{2,1,0:T(8,128)(2,1)}, bf16[4,32,40]{2,1,0:T(8,128)(2,1)}, f32[4,2816]{1,0:T(4,128)}, f32[1,2816]{1,0:T(1,128)}, f32[1,40]{1,0:...) custom-call(s32[4,2]{1,0:T(4,128)} %copy.19.pack_ref, bf16[4,32,2944]{2,1,0:T(8,128)(2,1)} %get-tuple-element.62.ret_ref, ...), custom_call_target="tpu_custom_call" | custom-call | tf_op jit(solution)/shard_map/pallas_call | solution.py:699
  126.9 1.4 %copy.21 = bf16[1,128,40]{1,2,0:T(8,128)(2,1)} copy(bf16[1,128,40]{2,1,0:T(8,128)(2,1)} %bitcast.17) | data formatting | bytes 20480
  128.4 1.3 %reduce = f32[2816]{0:T(1024)} reduce(f32[1,2816]{1,0:T(1,128)} %get-tuple-element.68, f32[]{:T(128)} %constant.14), dimensions={0}, to_apply=%get-tuple-element.68.reduce_sub_computation | reduce | bytes 22532 | tf_op jit(solution)/shard_map/pallas_call | solution.py:699

commit v2 on v1

--- a/solution.py
+++ b/solution.py
@@ -12,7 +12,7 @@
 LANES = 128
 PAD = 8
 WIDE = 256
-LAG = 2
+LAG = 3
 VMEM_LIMIT = 56 * 1024 * 1024
 HIGH = lax.Precision.HIGHEST
 
@@ -38,39 +38,33 @@
 def arrange_kernel(pack_ref, rows_ref, dt_ref, send_ref, tail_ref, tag_ref):
     held, block, width = send_ref.shape
     channels = rows_ref.shape[2]
-    heads = dt_ref.shape[2]
+    heads = dt_ref.shape[0]
+    steps = jnp.transpose(dt_ref[...].astype(F32))
     for j in range(held):
-        to = pack_ref[j, 0]
+        to = pack_ref[0, j]
         send_ref[to, :, :channels] = rows_ref[j]
         send_ref[to, :, channels:] = jnp.zeros((block, width - channels), BF16)
-        send_ref[to, :, channels : channels + heads] = dt_ref[j]
+        send_ref[to, :, channels : channels + heads] = steps[j * block : (j + 1) * block].astype(BF16)
         tail_ref[to] = rows_ref[j, block - 2 * PAD :, :].astype(F32)[PAD:].astype(BF16)
-        tag_ref[to] = jnp.full((8, LANES), pack_ref[j, 1], jnp.int32)
-
-
-def peers_barrier(seq_axis_peers, groups, me_s, me_d, n_seq):
-    barrier = pltpu.get_barrier_semaphore()
-
-    def tell(s, d):
-        pl.semaphore_signal(
-            barrier, inc=1, device_id={"seq": s, "dp": d}, device_id_type=pl.DeviceIdType.MESH
-        )
-
-    for k in range(1, groups):
-        tell(me_s, lax.rem(me_d + k, groups))
-    for step in (1, -1):
-        ok = (me_s + step >= 0) & (me_s + step < n_seq)
-
-        @pl.when(ok)
-        def _():
-            for d in range(groups if seq_axis_peers == "all" else 0):
-                tell(me_s + step, d)
-
-    pl.semaphore_wait(barrier, groups - 1 + groups * sides(me_s, n_seq))
-
-
-def sides(me, count):
-    return (me > 0).astype(jnp.int32) + (me < count - 1).astype(jnp.int32)
+        tag_ref[to] = jnp.full((8, LANES), pack_ref[1, j], jnp.int32)
+
+
+def home(s, d, n_seq, groups):
+    if (n_seq, groups) != (8, 4):
+        return s, d
+    sp, dp = lax.rem(s, 2), lax.rem(d, 2)
+    return s - sp + dp, d - dp + sp
+
+
+def tell(s, d):
+    pl.semaphore_signal(
+        pltpu.get_barrier_semaphore(), inc=1, device_id={"seq": s, "dp": d},
+        device_id_type=pl.DeviceIdType.MESH,
+    )
+
+
+def one_if(cond):
+    return jnp.where(cond, 1, 0).astype(jnp.int32)
 
 
 def remote(src, dst, ssem, rsem, s, d):
@@ -86,61 +80,133 @@
 
 def spread_kernel(
     n_seq, groups,
-    send_ref, tail_ref, tag_ref, reset_ref,
-    got_ref, gtag_ref, ptail_ref, ptag_ref, preset_ref,
-    ss, rs, tss, trs, qss, qrs, uss, urs, wss, wrs, lsem,
+    send_ref, tail_ref, tag_ref, reset_ref, gout_ref,
+    got_ref, gtag_ref, ptail_ref, ptag_ref, preset_ref, oreset_ref, ogout_ref,
+    ss, rs, tss, trs, qss, qrs, uss, urs, wss, wrs,
 ):
     me_s, me_d = lax.axis_index("seq"), lax.axis_index("dp")
-    peers_barrier("all", groups, me_s, me_d, n_seq)
-    row_copies = []
-    for k in range(1, groups):
-        d = lax.rem(me_d + k, groups)
-        a = remote(send_ref.at[d], got_ref.at[me_d], ss.at[k], rs.at[k], me_s, d)
-        b = remote(tag_ref.at[d], gtag_ref.at[me_d], tss.at[k], trs.at[k], me_s, d)
-        a.start()
-        b.start()
-        row_copies += [a, b]
-    own = [
-        pltpu.make_async_copy(send_ref.at[me_d], got_ref.at[me_d], lsem.at[0]),
-        pltpu.make_async_copy(tag_ref.at[me_d], gtag_ref.at[me_d], lsem.at[1]),
-    ]
-    for c in own:
-        c.start()
-
-    def tails():
-        out = []
+    vs, vd = home(me_s, me_d, n_seq, groups)
+
+    for j in range(groups):
+
+        @pl.when((vs != me_s) | (j != me_d))
+        def _():
+            tell(vs, j)
+
+        @pl.when((vs > 0) & ((vs - 1 != me_s) | (j != me_d)))
+        def _():
+            tell(vs - 1, j)
+
+    after = me_s + 1 < n_seq
+    count = groups - one_if(vs == me_s)
+    count = count + jnp.where(after, groups - one_if(vs == me_s + 1), 0)
+    pl.semaphore_wait(pltpu.get_barrier_semaphore(), count)
+
+    def to_all(shard, pairs_of, act):
         for k in range(groups):
-            d = lax.rem(me_d + k, groups)
-            out.append(remote(tail_ref.at[d], ptail_ref.at[me_d], qss.at[k], qrs.at[k], me_s + 1, d))
-            out.append(remote(tag_ref.at[d], ptag_ref.at[me_d], uss.at[k], urs.at[k], me_s + 1, d))
-        out.append(remote(reset_ref, preset_ref, wss, wrs, me_s + 1, me_d))
-        return out
-
-    @pl.when(me_s + 1 < n_seq)
+            g = lax.rem(me_d + k, groups)
+            s, d = home(shard, g, n_seq, groups)
+            mine = (s == me_s) & (d == me_d)
+            pairs = pairs_of(g)
+
+            @pl.when(mine)
+            def _():
+                for n, (src, dst, ssem, rsem) in enumerate(pairs):
+                    act(pltpu.make_async_copy(src, dst, ssem), True)
+
+            @pl.when(jnp.logical_not(mine))
+            def _():
+                for src, dst, ssem, rsem in pairs:
+                    act(remote(src, dst, ssem, rsem, s, d), False)
+
+    def heads_of(g):
+        return [
+            (tag_ref.at[g], gtag_ref.at[me_d], tss.at[g], trs.at[me_d]),
+            (send_ref.at[g], got_ref.at[me_d], ss.at[g], rs.at[me_d]),
+        ]
+
+    def tails_of(g):
+        return [
+            (tag_ref.at[g], ptag_ref.at[me_d], uss.at[g], urs.at[me_d]),
+            (tail_ref.at[g], ptail_ref.at[me_d], qss.at[g], qrs.at[me_d]),
+        ]
+
+    def own_values(act):
+        s, d = vs, vd
+        mine = (s == me_s) & (d == me_d)
+        pairs = [
+            (reset_ref, oreset_ref, wss.at[0], wrs.at[0]),
+            (gout_ref, ogout_ref, wss.at[1], wrs.at[1]),
+        ]
+
+        @pl.when(mine)
+        def _():
+            for src, dst, ssem, rsem in pairs:
+                act(pltpu.make_async_copy(src, dst, ssem), True)
+
+        @pl.when(jnp.logical_not(mine))
+        def _():
+            for src, dst, ssem, rsem in pairs:
+                act(remote(src, dst, ssem, rsem, s, d), False)
+
+    def next_reset(act):
+        s, d = home(me_s + 1, me_d, n_seq, groups)
+        mine = (s == me_s) & (d == me_d)
+
+        @pl.when(mine)
+        def _():
+            act(pltpu.make_async_copy(reset_ref, preset_ref, wss.at[2]), True)
+
+        @pl.when(jnp.logical_not(mine))
+        def _():
+            act(remote(reset_ref, preset_ref, wss.at[2], wrs.at[2], s, d), False)
+
+    start = lambda c, local: c.start()
+    sent = lambda c, local: c.wait() if local else c.wait_send()
+    to_all(me_s, heads_of, start)
+
+    @pl.when(after)
     def _():
-        for c in tails():
-            c.start()
-
-    @pl.when(me_s == 0)
+        to_all(me_s + 1, tails_of, start)
+        next_reset(start)
+
+    own_values(start)
+
+    @pl.when(vs == 0)
     def _():
         ptail_ref[...] = jnp.zeros(ptail_ref.shape, BF16)
         ptag_ref[...] = jnp.zeros(ptag_ref.shape, jnp.int32)
         preset_ref[...] = jnp.zeros(preset_ref.shape, jnp.int32)
 
-    for c in own:
-        c.wait()
-    for c in row_copies:
-        c.wait()
-
-    @pl.when(me_s + 1 < n_seq)
+    for j in range(groups):
+
+        @pl.when((vs != me_s) | (j != me_d))
+        def _():
+            remote(tag_ref.at[j], gtag_ref.at[j], tss.at[j], trs.at[j], vs, j).wait_recv()
+            remote(send_ref.at[j], got_ref.at[j], ss.at[j], rs.at[j], vs, j).wait_recv()
+
+        @pl.when((vs > 0) & ((vs - 1 != me_s) | (j != me_d)))
+        def _():
+            remote(tag_ref.at[j], ptag_ref.at[j], uss.at[j], urs.at[j], vs - 1, j).wait_recv()
+            remote(tail_ref.at[j], ptail_ref.at[j], qss.at[j], qrs.at[j], vs - 1, j).wait_recv()
+
+    @pl.when((vs != me_s) | (vd != me_d))
     def _():
-        for c in tails():
-            c.wait_send()
-
-    @pl.when(me_s > 0)
+        remote(reset_ref, oreset_ref, wss.at[0], wrs.at[0], vs, vd).wait_recv()
+        remote(gout_ref, ogout_ref, wss.at[1], wrs.at[1], vs, vd).wait_recv()
+
+    @pl.when((vs > 0) & ((vs - 1 != me_s) | (vd != me_d)))
     def _():
-        for c in tails():
-            c.wait_recv()
+        remote(reset_ref, preset_ref, wss.at[2], wrs.at[2], vs - 1, vd).wait_recv()
+
+    to_all(me_s, heads_of, sent)
+
+    @pl.when(after)
+    def _():
+        to_all(me_s + 1, tails_of, sent)
+        next_reset(sent)
+
+    own_values(sent)
 
 
 def token_values(dtp, bias_row, rate_row, reset_row):
@@ -167,6 +233,11 @@
     decay = jnp.where(seg_last == 0.0, jnp.exp(last), 0.0)
     allowed = (t_i >= s_i) & (seg_col == seg_row)
     return raw, size, cum, cum_t, weight, entry, decay, allowed, reset_col
+
+
+def lane_row(ref):
+    values = ref[...].reshape(1, -1)
+    return jnp.concatenate([values, jnp.zeros((1, LANES - values.shape[1]), F32)], axis=1)
 
 
 def pair(x, i, head_size, rows):
@@ -198,8 +269,9 @@
         prior = jnp.where(ptag_ref[g, 0, 0] == held - 1, ptail_ref[g].astype(F32), prior)
     ext_ref[0:PAD, :] = prior
 
+    rate = lane_row(rate_ref)
     raw, size, cum, cum_t, wgt, ent, dec, allowed, reset_col = token_values(
-        dtp_ref[...], sbias_ref[...], rate_ref[...], reset_ref[...]
+        dtp_ref[...], lane_row(sbias_ref), rate, reset_ref[...]
     )
     prev = jnp.broadcast_to(preset_ref[...].astype(F32), (PAD, length))
     pick = iota((PAD, length), 1) == iota((PAD, length), 0) + (length - PAD)
@@ -215,7 +287,7 @@
     join_ref[2] = j3
     for lo in range(0, channels, LANES):
         sl = slice(lo, lo + LANES)
-        v = cbias_ref[:, sl] + weight_ref[3:4, sl] * ext_ref[PAD:, sl]
+        v = cbias_ref[sl].reshape(1, LANES) + weight_ref[3:4, sl] * ext_ref[PAD:, sl]
         v = v + weight_ref[2:3, sl] * (ext_ref[PAD - 1 : PAD - 1 + length, sl] * j1)
         v = v + weight_ref[1:2, sl] * (ext_ref[PAD - 2 : PAD - 2 + length, sl] * j2)
         v = v + weight_ref[0:1, sl] * (ext_ref[PAD - 3 : PAD - 3 + length, sl] * j3)
@@ -236,26 +308,23 @@
 
 
 def chain_kernel(
-    n_seq, state_ref, gstate_ref, decay_ref, enter_ref, after_ref,
+    n_seq, groups, state_ref, gstate_ref, decay_ref, enter_ref, after_ref,
     fout, bout, fin, bin_, fss, frs, bss, brs,
 ):
-    me, me_d = lax.axis_index("seq"), lax.axis_index("dp")
+    me, seq = home(lax.axis_index("seq"), lax.axis_index("dp"), n_seq, groups)
     pieces = state_ref.shape[0]
-    barrier = pltpu.get_barrier_semaphore()
     for step in (1, -1):
-        ok = (me + step >= 0) & (me + step < n_seq)
-
-        @pl.when(ok)
-        def _():
-            pl.semaphore_signal(
-                barrier, inc=1, device_id={"seq": me + step, "dp": me_d},
-                device_id_type=pl.DeviceIdType.MESH,
-            )
-
-    pl.semaphore_wait(barrier, sides(me, n_seq))
+
+        @pl.when((me + step >= 0) & (me + step < n_seq))
+        def _():
+            tell(*home(me + step, seq, n_seq, groups))
+
+    pl.semaphore_wait(
+        pltpu.get_barrier_semaphore(), one_if(me > 0) + one_if(me < n_seq - 1)
+    )
 
     def one(c, first, final, local, got, out, result, ssem, rsem, to):
-        copy = remote(out.at[c], got.at[c], ssem.at[c], rsem.at[c], to, me_d)
+        copy = remote(out.at[c], got.at[c], ssem.at[c], rsem.at[c], *home(to, seq, n_seq, groups))
 
         @pl.when(first)
         def _():
@@ -291,11 +360,11 @@
     def drain(c, carry):
         @pl.when(me < n_seq - 1)
         def _():
-            remote(fout.at[c], fin.at[c], fss.at[c], frs.at[c], me + 1, me_d).wait_send()
+            remote(fout.at[c], fin.at[c], fss.at[c], frs.at[c], *home(me + 1, seq, n_seq, groups)).wait_send()
 
         @pl.when(me > 0)
         def _():
-            remote(bout.at[c], bin_.at[c], bss.at[c], brs.at[c], me - 1, me_d).wait_send()
+            remote(bout.at[c], bin_.at[c], bss.at[c], brs.at[c], *home(me - 1, seq, n_seq, groups)).wait_send()
 
         return carry
 
@@ -319,10 +388,11 @@
     length, channels = act_ref.shape
     groups, block, _ = back_ref.shape
     per = LANES // head_size
+    rate = lane_row(rate_ref)
     raw, size, cum, cum_t, wgt, ent, dec, allowed, _ = token_values(
-        dtp_ref[...], sbias_ref[...], rate_ref[...], reset_ref[...]
-    )
-    gain = gain_ref[...]
+        dtp_ref[...], lane_row(sbias_ref), rate, reset_ref[...]
+    )
+    gain = lane_row(gain_ref)
     b_rows = act_ref[:, inner : inner + n_state]
     c_rows = act_ref[:, inner + n_state :]
     scores = dot(c_rows, b_rows, ((1,), (1,)))
@@ -397,7 +467,7 @@
     is_last = iota((length, LANES), 0) == length - 1
     dcum = dcum_ref[...] + jnp.where(is_last, tot_ref[0:1, :], 0.0)
     dlog = dot((s_i >= t_i).astype(F32), dcum, precision=HIGH)
-    dsize = dsize_ref[...] - dlog * rate_ref[...]
+    dsize = dsize_ref[...] - dlog * rate
     draw = dsize * jax.nn.sigmoid(raw)
     gdt_ref[...] = draw
     param_ref[...] = jnp.zeros(param_ref.shape, F32)
@@ -433,32 +503,37 @@
 
 def return_kernel(
     n_seq, groups,
-    back_ref, spill_ref, param_ref,
-    ret_ref, rspill_ref, total_ref,
+    back_ref, spill_ref, param_ref, out_ref,
+    ret_ref, rspill_ref, total_ref, oout_ref,
     part, mid, fin,
-    ss, rs, qss, qrs, ass, ars, bss, brs, css, crs, lsem,
+    ss, rs, qss, qrs, ass, ars, bss, brs, css, crs, oss, ors,
 ):
     me_s, me_d = lax.axis_index("seq"), lax.axis_index("dp")
-    barrier = pltpu.get_barrier_semaphore()
-
-    def tell(s, d):
-        pl.semaphore_signal(
-            barrier, inc=1, device_id={"seq": s, "dp": d}, device_id_type=pl.DeviceIdType.MESH
-        )
-
+    vs, vd = home(me_s, me_d, n_seq, groups)
+    after = me_s + 1 < n_seq
+
+    for g in range(groups):
+        s, d = home(me_s, g, n_seq, groups)
+
+        @pl.when((s != me_s) | (d != me_d))
+        def _():
+            tell(s, d)
+
+        @pl.when(after)
+        def _():
+            s1, d1 = home(me_s + 1, g, n_seq, groups)
+
+            @pl.when((s1 != me_s) | (d1 != me_d))
+            def _():
+                tell(s1, d1)
+
+    for k in range(1, n_seq):
+        tell(lax.rem(me_s + k, n_seq), me_d)
     for k in range(1, groups):
         tell(me_s, lax.rem(me_d + k, groups))
-    for k in range(1, n_seq):
-        tell(lax.rem(me_s + k, n_seq), me_d)
-    for step in (1, -1):
-        ok = (me_s + step >= 0) & (me_s + step < n_seq)
-
-        @pl.when(ok)
-        def _():
-            for k in range(1, groups):
-                tell(me_s + step, lax.rem(me_d + k, groups))
-
-    pl.semaphore_wait(barrier, groups + n_seq - 2 + (groups - 1) * sides(me_s, n_seq))
+    count = groups - one_if(vs == me_s) + n_seq - 1 + groups - 1
+    count = count + jnp.where(vs > 0, groups - one_if(vs - 1 == me_s), 0)
+    pl.semaphore_wait(pltpu.get_barrier_semaphore(), count)
 
     scatter = []
     for k in range(1, n_seq):
@@ -466,28 +541,35 @@
         scatter.append(remote(param_ref.at[s], part.at[k], ass.at[k], ars.at[k], s, me_d))
     for c in scatter:
         c.start()
-    rows = []
-    for k in range(1, groups):
-        d = lax.rem(me_d + k, groups)
-        rows.append(remote(back_ref.at[d], ret_ref.at[me_d], ss.at[k], rs.at[k], me_s, d))
-    for c in rows:
-        c.start()
-    own = pltpu.make_async_copy(back_ref.at[me_d], ret_ref.at[me_d], lsem)
-    own.start()
-
-    def spills():
-        return [
-            remote(
-                spill_ref, rspill_ref.at[me_d], qss.at[k], qrs.at[k], me_s - 1,
-                lax.rem(me_d + k, groups),
-            )
-            for k in range(groups)
-        ]
-
-    @pl.when(me_s > 0)
-    def _():
-        for c in spills():
-            c.start()
+
+    def move(src, dst, ssem, rsem, s, d, act):
+        mine = (s == me_s) & (d == me_d)
+
+        @pl.when(mine)
+        def _():
+            act(pltpu.make_async_copy(src, dst, ssem), True)
+
+        @pl.when(jnp.logical_not(mine))
+        def _():
+            act(remote(src, dst, ssem, rsem, s, d), False)
+
+    def rows(act):
+        for k in range(groups):
+            j = lax.rem(me_d + k, groups)
+            move(back_ref.at[j], ret_ref.at[vd], ss.at[j], rs.at[vd], vs, j, act)
+
+    def spills(act):
+        @pl.when(vs > 0)
+        def _():
+            for j in range(groups):
+                move(spill_ref, rspill_ref.at[vd], qss.at[j], qrs.at[vd], vs - 1, j, act)
+
+    def outs(act):
+        move(out_ref, oout_ref, oss, ors, vs, vd, act)
+
+    start = lambda c, local: c.start()
+    sent = lambda c, local: c.wait() if local else c.wait_send()
+    spills(start)
 
     @pl.when(me_s == n_seq - 1)
     def _():
@@ -505,6 +587,8 @@
     ]
     for c in across:
         c.start()
+    rows(start)
+    outs(start)
     for c in across:
         c.wait()
     total = jnp.zeros(mine.shape, F32)
@@ -518,48 +602,57 @@
     ]
     for c in gather:
         c.start()
-    for c in rows:
-        c.wait()
-    own.wait()
-
-    @pl.when(me_s > 0)
+
+    for g in range(groups):
+        s, d = home(me_s, g, n_seq, groups)
+
+        @pl.when((s != me_s) | (d != me_d))
+        def _():
+            remote(back_ref.at[g], ret_ref.at[g], ss.at[g], rs.at[g], s, d).wait_recv()
+
+        s1, d1 = home(me_s + 1, g, n_seq, groups)
+
+        @pl.when(after & ((s1 != me_s) | (d1 != me_d)))
+        def _():
+            remote(spill_ref, rspill_ref.at[g], qss.at[g], qrs.at[g], s1, d1).wait_recv()
+
+    @pl.when((vs != me_s) | (vd != me_d))
     def _():
-        for c in spills():
-            c.wait_send()
-
-    @pl.when(me_s < n_seq - 1)
-    def _():
-        for c in spills():
-            c.wait_recv()
-
+        remote(out_ref, oout_ref, oss, ors, vs, vd).wait_recv()
+
+    rows(sent)
+    spills(sent)
+    outs(sent)
     for c in gather:
         c.wait()
 
 
 def place_kernel(
-    share, pack_ref, ret_ref, rspill_ref, total_ref,
-    gin_ref, gdt_ref, gw_ref, gb_ref, gsb_ref, grate_ref, ggain_ref,
+    share, pack_ref, ret_ref, rspill_ref, total_ref, oout_ref,
+    gin_ref, gdt_ref, gw_ref, gb_ref, gsb_ref, grate_ref, ggain_ref, out_ref, steps_ref,
 ):
     held, block, channels = gin_ref.shape
-    heads = gdt_ref.shape[2]
+    heads = gdt_ref.shape[0]
+    out_ref[...] = oout_ref[...]
     for j in range(held):
-        g = pack_ref[j, 0]
+        g = pack_ref[0, j]
         gin_ref[j] = ret_ref[g, :, :channels]
-        gdt_ref[j] = ret_ref[g, :, channels : channels + heads]
+        steps_ref[j * block : (j + 1) * block, :] = ret_ref[g, :, channels:].astype(F32)
         low = ret_ref[g, block - 2 * PAD :, :channels].astype(F32)
         extra = rspill_ref[g].astype(F32)
-        last = pack_ref[j, 1] == held - 1
+        last = pack_ref[1, j] == held - 1
         extra = jnp.where(last, extra, 0.0)
         gin_ref[j, block - 2 * PAD :, :] = jnp.concatenate(
             [low[:PAD], low[PAD:] + extra], axis=0
         ).astype(BF16)
+    gdt_ref[...] = jnp.transpose(steps_ref[...])[:heads].astype(BF16)
     for lo in range(0, channels, LANES):
         at, off = divmod(lo, share)
         gw_ref[:, lo : lo + LANES] = total_ref[at, 0:4, off : off + LANES]
-        gb_ref[:, lo : lo + LANES] = total_ref[at, 4:5, off : off + LANES]
-    gsb_ref[...] = total_ref[0, 5:6, 0:heads]
-    grate_ref[...] = total_ref[0, 6:7, 0:heads]
-    ggain_ref[...] = total_ref[0, 7:8, 0:heads]
+        gb_ref[lo : lo + LANES] = total_ref[at, 4, off : off + LANES]
+    gsb_ref[...] = total_ref[0, 5, 0:heads]
+    grate_ref[...] = total_ref[0, 6, 0:heads]
+    ggain_ref[...] = total_ref[0, 7, 0:heads]
 
 
 def shape(dims, kind):
@@ -591,10 +684,8 @@
     held = packing.shape[1]
     block = length // held
     width = channels + LANES
-    pack = packing[0]
+    pack = jnp.transpose(packing[0])
     dma = pltpu.SemaphoreType.DMA
-    row = lambda a: a.reshape(1, -1)
-    padded = lambda a: jnp.pad(row(a), ((0, 0), (0, LANES - heads)))
 
     send, tail, tag = call(
         arrange_kernel,
@@ -604,23 +695,24 @@
             shape((groups, PAD, channels), BF16),
             shape((groups, 8, LANES), jnp.int32),
         ),
-    )(pack, conv_input[0].reshape(held, block, channels), dt_raw[0].reshape(held, block, heads))
-
-    got, gtag, ptail, ptag, preset = call(
+    )(pack, conv_input[0].reshape(held, block, channels), jnp.transpose(dt_raw[0]))
+
+    got, gtag, ptail, ptag, preset, oreset, gout = call(
         functools.partial(spread_kernel, n_seq, groups),
-        [vmem()] * 4,
+        [vmem()] * 5,
         (
             shape((groups, block, width), BF16),
             shape((groups, 8, LANES), jnp.int32),
             shape((groups, PAD, channels), BF16),
             shape((groups, 8, LANES), jnp.int32),
             shape((1, length), jnp.int32),
+            shape((1, length), jnp.int32),
+            shape((length, inner), BF16),
         ),
-        [dma((groups,))] * 8 + [dma, dma, dma((2,))],
+        [dma((groups,))] * 8 + [dma((3,)), dma((3,))],
         cid=0,
-    )(send, tail, tag, resets)
-
-    sbias, rate, gain = padded(dt_bias), padded(decay_rate), padded(skip_gain)
+    )(send, tail, tag, resets, grad_out[0])
+
     pieces = inner // WIDE
     state_shape = shape((pieces, n_state, WIDE), BF16)
     ext, act, slope, dtp, join, state, gstate, decay = call(
@@ -637,12 +729,11 @@
             shape((pieces, 8, WIDE), F32),
         ),
     )(
-        gtag[:, :1, :1], ptag[:, :1, :1], got, ptail, resets, preset, conv_weight, row(conv_bias),
-        sbias, rate, grad_out[0],
+        gtag, ptag, got, ptail, oreset, preset, conv_weight, conv_bias, dt_bias, decay_rate, gout,
     )
 
     enter, after = call(
-        functools.partial(chain_kernel, n_seq),
+        functools.partial(chain_kernel, n_seq, groups),
         [vmem()] * 3,
         (state_shape, state_shape),
         [pltpu.VMEM(state_shape.shape, BF16)] * 4 + [dma((pieces,))] * 4,
@@ -671,17 +762,18 @@
             pltpu.VMEM((16, LANES), F32),
         ],
     )(
-        gtag[:, :1, :1], ext, act, slope, dtp, join, enter, after, resets, conv_weight, sbias, rate,
-        gain, grad_out[0],
-    )
-
-    ret, rspill, total = call(
+        gtag, ext, act, slope, dtp, join, enter, after, oreset, conv_weight, dt_bias, decay_rate,
+        skip_gain, gout,
+    )
+
+    ret, rspill, total, oout = call(
         functools.partial(return_kernel, n_seq, groups),
-        [vmem()] * 3,
+        [vmem()] * 4,
         (
             shape((groups, block, width), BF16),
             shape((groups, PAD, channels), BF16),
             params,
+            shape((length, inner), BF16),
         ),
         [
             pltpu.VMEM((n_seq, 8, share), F32),
@@ -692,32 +784,34 @@
         + [dma((n_seq,))] * 2
         + [dma((groups,))] * 2
         + [dma((n_seq,))] * 2
-        + [dma],
+        + [dma, dma],
         cid=2,
-    )(back, spill, param)
-
-    gin, gdt, gw, gb, gsb, grate, ggain = call(
+    )(back, spill, param, out)
+
+    gin, gdt, gw, gb, gsb, grate, ggain, layer_out = call(
         functools.partial(place_kernel, share),
-        [smem()] + [vmem()] * 3,
+        [smem()] + [vmem()] * 4,
         (
             shape((held, block, channels), BF16),
-            shape((held, block, heads), BF16),
+            shape((heads, length), BF16),
             shape((4, channels), F32),
-            shape((1, channels), F32),
-            shape((1, heads), F32),
-            shape((1, heads), F32),
-            shape((1, heads), F32),
+            shape((channels,), F32),
+            shape((heads,), F32),
+            shape((heads,), F32),
+            shape((heads,), F32),
+            shape((length, inner), BF16),
         ),
-    )(pack, ret, rspill, total)
+        [pltpu.VMEM((length, LANES), F32)],
+    )(pack, ret, rspill, total, oout)
     return (
-        out[None],
+        layer_out[None],
         gin.reshape(1, length, channels),
-        gdt.reshape(1, length, heads),
+        jnp.transpose(gdt)[None],
         gw,
-        gb[0],
-        gsb[0],
-        grate[0],
-        ggain[0],
+        gb,
+        gsb,
+        grate,
+        ggain,
     )
 
 

time: 130 us -> 104 us (0.80)
  Pallas kernels: 116 us -> 103 us
  local copies, waits for them, and re-layouts: 11.6 us -> 0 us
  other arithmetic: 1.33 us -> 0 us
    pallas_call x4, Pallas kernels: 94.9 us -> 82.2 us  [the longest x1 32.2 us: per_device(): call(functools.partial(chain_kernel, n_seq, groups), [vmem()] * 3, (state...]
    pad x3 -> x0, local copies, waits for them, and re-layouts: 3.51 us -> none  [per_device(): padded = lambda a: jnp.pad(row(a), ((0, 0), (0, LANES - heads)))]
    unnamed x2 -> x0, local copies, waits for them, and re-layouts: 2.85 us -> none
    slice x2 -> x0, local copies, waits for them, and re-layouts: 2.61 us -> none  [the longest x1 1.31 us: per_device(): gtag[:, :1, :1]]
    squeeze x1 -> x0, local copies, waits for them, and re-layouts: 1.34 us -> none  [per_device(): pack = packing[0]]
    pallas_call x1 -> x0, other arithmetic: 1.33 us -> none  [per_device(): call(functools.partial(place_kernel, share), [smem()] + [vmem()] * 3, (sh...]
    reshape x1 -> x0, local copies, waits for them, and re-layouts: 1.31 us -> none  [per_device(): row = lambda a: a.reshape(1, -1)]
where the time goes in v2:
time: 104 us
  Pallas kernels  103 us (99%)
    pallas_call x1, Pallas kernels, per_device(): call(functools.partial(chain_kernel, n_seq, groups), [vmem()] * 3, (state...  32.2 us
    pallas_call x1, Pallas kernels, per_device(): call(functools.partial(return_kernel, n_seq, groups), [vmem()] * 4, (shap...  29 us
    pallas_call x1, Pallas kernels, per_device(): call(functools.partial(spread_kernel, n_seq, groups), [vmem()] * 5, (shap...  18.4 us
    pallas_call x1, Pallas kernels, per_device(): call(functools.partial(back_kernel, inner, head_size, n_state, heads, sha...  12.4 us
    pallas_call x1, Pallas kernels, per_device(): call(functools.partial(front_kernel, inner, head_size, n_state), [smem(),...  6.51 us
    pallas_call x1, Pallas kernels, per_device(): call(functools.partial(place_kernel, share), [smem()] + [vmem()] * 4, (sh...  2.65 us
    pallas_call x1, Pallas kernels, per_device(): call(arrange_kernel, [smem(), vmem(), vmem()], (shape((groups, block, wid...  2.12 us

profile of v2, /device:TPU:0, one launch (start us, length us, event | category | flops | bytes accessed | tf_op | source)
XLA Modules:
  0.0 103.9 jit_solution(1628541291471437316)
XLA Ops:
  0.6 2.1 %shard_map.161 = (bf16[4,32,2944]{2,1,0:T(8,128)(2,1)}, bf16[4,8,2816]{2,1,0:T(8,128)(2,1)}, s32[4,8,128]{2,1,0:T(8,128)}) custom-call(s32[2,4]{1,0:T(2,128)} %bitcast.16, bf16[4,32,2816]{2,1,0:T(8,128)(2,1)} %bitcast.13, bf16[40,128]{1,0:T(8,128)(2,1)} %bitcast.15), custom_call_target="tpu_custom_call" | custom-call | tf_op jit(solution)/shard_map/pallas_call | solution.py:690
  2.8 18.4 %shard_map.162 = (bf16[4,32,2944]{2,1,0:T(8,128)(2,1)}, s32[4,8,128]{2,1,0:T(8,128)}, bf16[4,8,2816]{2,1,0:T(8,128)(2,1)}, s32[4,8,128]{2,1,0:T(8,128)}, s32[1,1...) custom-call(bf16[4,32,2944]{2,1,0:T(8,128)(2,1)} %get-tuple-element.44.send_ref, ...), custom_call_target="tpu_custom_call" | custom-call | tf_op jit(solution)/shard_map/pallas_call | solution.py:700
  21.1 6.5 %shard_map.163 = (f32[136,2816]{1,0:T(8,128)}, bf16[128,2816]{1,0:T(8,128)(2,1)}, f32[128,2816]{1,0:T(8,128)}, f32[128,128]{1,0:T(8,128)}, f32[3,128,128]{2,1,0:...) custom-call(s32[4,8,128]{2,1,0:T(8,128)} %get-tuple-element.47.tag_ref, ...), custom_call_target="tpu_custom_call" | custom-call | tf_op jit(solution)/shard_map/pallas_call | solution.py:718
  27.6 32.2 %shard_map.164 = (bf16[10,128,256]{2,1,0:T(8,128)(2,1)}, bf16[10,128,256]{2,1,0:T(8,128)(2,1)}) custom-call(bf16[10,128,256]{2,1,0:T(8,128)(2,1)} %get-tuple-element.59.state_ref, bf16[10,128,256]{2,1,0:T(8,128)(2,1)} %get-tuple-element.60.gstate_ref, f32[10,8,256]{2,1,0:T(8,128)} %get-tuple-element.61.decay_ref), custom_call_target="tpu_custom_call" | custom-call | tf_op jit(solution)/shard_map/pallas_call | solution.py:735
  59.8 12.4 %shard_map.165 = (bf16[128,2560]{1,0:T(8,128)(2,1)}, bf16[4,32,2944]{2,1,0:T(8,128)(2,1)}, bf16[8,2816]{1,0:T(8,128)(2,1)}, f32[8,8,384]{2,1,0:T(8,128)}) custom-call(s32[4,8,128]{2,1,0:T(8,128)} %get-tuple-element.47.tag_ref, f32[136,2816]{1,0:T(8,128)} %get-tuple-element.54.ext_ref, bf16[128,2816]{1,0:T(8,128)(2,1)} %get-tuple-element.55.act_ref, ...), custom_call_target="tpu_custom_call" | custom-call | tf_op jit(solution)/shard_map/pallas_call | solution.py:746
  72.2 29.0 %shard_map.166 = (bf16[4,32,2944]{2,1,0:T(8,128)(2,1)}, bf16[4,8,2816]{2,1,0:T(8,128)(2,1)}, f32[8,8,384]{2,1,0:T(8,128)}, bf16[128,2560]{1,0:T(8,128)(2,1)}) custom-call(bf16[4,32,2944]{2,1,0:T(8,128)(2,1)} %get-tuple-element.64.back_ref, bf16[8,2816]{1,0:T(8,128)(2,1)} %get-tuple-element.65.spill_ref, f32[8,8,384]{2,1,0:T(8,128)} %get-tuple-element.66.param_ref, ...), custom_call_target="tpu_custom_call" | custom-call | tf_op jit(solution)/shard_map/pallas_call | solution.py:769
  101.2 2.6 %shard_map.167 = (bf16[4,32,2816]{2,1,0:T(8,128)(2,1)}, bf16[40,128]{1,0:T(8,128)(2,1)}, f32[4,2816]{1,0:T(4,128)}, f32[2816]{0:T(1024)}, f32[40]{0:T(128)}, /*i...) custom-call(s32[2,4]{1,0:T(2,128)} %bitcast.17, bf16[4,32,2944]{2,1,0:T(8,128)(2,1)} %get-tuple-element.68.ret_ref, ...), custom_call_target="tpu_custom_call" | custom-call | tf_op jit(solution)/shard_map/pallas_call | solution.py:791
